TPU v7x, 32 devices: a whole 2x2x4 slice. The times are simulated.
32 devices in a mesh: dp: 8 (over y, x, core), mp: 4 (over z).
Axes of the slice: x: 2, y: 2, z: 4, core: 2. Of those that a mesh axis runs over, the one named last changes fastest.
Arguments:
- tokens: bfloat16 [8192, 1152], P('dp'), may hold values from -6 to 6
- cotangent: bfloat16 [8192, 1152], P('dp'), may hold values from -6 to 6
- lengths: int32 [8], P('dp'), may hold values from 512 to 1024, as said below
- rates: float32 [6], replicated, as said below
- query_weight: float32 [1152, 1024], P('dp', 'mp'), may hold values from -0.1875 to 0.1875
- query_moment: float32 [1152, 1024], P('dp', 'mp'), may hold values from -256 to 256
- query_average: float32 [1152, 1024], P('dp', 'mp'), may hold values from -0.1875 to 0.1875
- output_weight: float32 [1024, 1152], P('mp', 'dp'), may hold values from -1.5 to 1.5
- output_moment: float32 [1024, 1152], P('mp', 'dp'), may hold values from -56 to 56
- output_average: float32 [1024, 1152], P('mp', 'dp'), may hold values from -1.5 to 1.5
- gating_weight: float32 [2, 1152, 6912], P(None, 'dp', 'mp'), may hold values from -0.1875 to 0.1875
- gating_moment: float32 [2, 1152, 6912], P(None, 'dp', 'mp'), may hold values from -128 to 128
- gating_average: float32 [2, 1152, 6912], P(None, 'dp', 'mp'), may hold values from -0.1875 to 0.1875
- down_weight: float32 [6912, 1152], P('mp', 'dp'), may hold values from -0.078125 to 0.078125
- down_moment: float32 [6912, 1152], P('mp', 'dp'), may hold values from -256 to 256
- down_average: float32 [6912, 1152], P('mp', 'dp'), may hold values from -0.078125 to 0.078125
- context_weight: float32 [2, 1152, 256], P(None, ('dp', 'mp')), may hold values from -0.1875 to 0.1875
- context_moment: float32 [2, 1152, 256], P(None, ('dp', 'mp')), may hold values from -512 to 512
- context_average: float32 [2, 1152, 256], P(None, ('dp', 'mp')), may hold values from -0.1875 to 0.1875
- gains_weight: float32 [2, 1152], P(None, ('dp', 'mp')), may hold values from 0.5 to 1.5
- gains_moment: float32 [2, 1152], P(None, ('dp', 'mp')), may hold values from -160 to 160
- gains_average: float32 [2, 1152], P(None, ('dp', 'mp')), may hold values from 0.5 to 1.5
Outputs:
- block_out: float32 [8192, 1152], P(('dp', 'mp'))
- tokens_grad: float32 [8192, 1152], P(('dp', 'mp'))
- query_grads: float32 [1152, 1024], P('dp', 'mp')
- query_moments: float32 [1152, 1024], P('dp', 'mp')
- query_averages: float32 [1152, 1024], P('dp', 'mp')
- query_updated: float32 [1152, 1024], P('dp', 'mp')
- output_grads: float32 [1024, 1152], P('mp', 'dp')
- output_moments: float32 [1024, 1152], P('mp', 'dp')
- output_averages: float32 [1024, 1152], P('mp', 'dp')
- output_updated: float32 [1024, 1152], P('mp', 'dp')
- gating_grads: float32 [2, 1152, 6912], P(None, 'dp', 'mp')
- gating_moments: float32 [2, 1152, 6912], P(None, 'dp', 'mp')
- gating_averages: float32 [2, 1152, 6912], P(None, 'dp', 'mp')
- gating_updated: float32 [2, 1152, 6912], P(None, 'dp', 'mp')
- down_grads: float32 [6912, 1152], P('mp', 'dp')
- down_moments: float32 [6912, 1152], P('mp', 'dp')
- down_averages: float32 [6912, 1152], P('mp', 'dp')
- down_updated: float32 [6912, 1152], P('mp', 'dp')
- context_grads: float32 [2, 1152, 256], P(None, ('dp', 'mp'))
- context_moments: float32 [2, 1152, 256], P(None, ('dp', 'mp'))
- context_averages: float32 [2, 1152, 256], P(None, ('dp', 'mp'))
- context_updated: float32 [2, 1152, 256], P(None, ('dp', 'mp'))
- gains_grads: float32 [2, 1152], P(None, ('dp', 'mp'))
- gains_moments: float32 [2, 1152], P(None, ('dp', 'mp'))
- gains_averages: float32 [2, 1152], P(None, ('dp', 'mp'))
- gains_updated: float32 [2, 1152], P(None, ('dp', 'mp'))
Inputs may be any that keep to these rules, and one draw needn't show every extreme that they name: `lengths`: the true token count of each sequence; slots at and after it are padding; at least one sequence fills all 1024 slots. `rates`: one positive learning rate per parameter kind.
All inputs are finite; a program needn't handle non-finite values.
Results may differ from a plain program's by a relative error of at most 0.014.
Values may be sent and summed in bfloat16 or wider, within the bound.
No kernel may reach another device: no remote copies, remote signals or barrier semaphores. Data moves between devices by JAX's collectives and lax.ppermute only.
A program may use at most 192 MiB of HBM per device.

v0:
```python
import jax
import jax.numpy as jnp
from jax import lax
from jax.experimental import pallas as pl
from jax.experimental.pallas import tpu as pltpu
from jax.sharding import PartitionSpec as P

HD = 256
LANES = 128
TILE = 256
VMEM_BYTES = 56 * 1024 * 1024
EPSILON = 1e-06
MOMENTUM = 0.9
AVERAGING = 0.5
BF = jnp.bfloat16
F32 = jnp.float32


def mm(a, b, dims):
    return lax.dot_general(a, b, (dims, ((), ())), preferred_element_type=F32)


def inverse_rms(tensor):
    return lax.rsqrt(jnp.mean(tensor * tensor, axis=-1, keepdims=True) + EPSILON)


def norm_back(grad_in, unit, inverse, gain_vec):
    scaled = grad_in * gain_vec
    return inverse * (scaled - unit * jnp.mean(scaled * unit, axis=-1, keepdims=True))


def rotation(length, head_size):
    halfway = head_size // 2
    frequency = 1000000.0 ** (-(jnp.arange(halfway).astype(F32) * 2.0 / head_size))
    angles = jnp.arange(length).astype(F32)[:, None] * frequency[None, :]
    return (jnp.cos(angles), jnp.sin(angles))


def rotate(tensor, cosine, sine_tab):
    halfway = tensor.shape[-1] // 2
    former = tensor[..., :halfway]
    latter = tensor[..., halfway:]
    return jnp.concatenate(
        [former * cosine - latter * sine_tab, latter * cosine + former * sine_tab], axis=-1
    )


def advance(gradient, moment, average, weight, step_rate):
    moment_new = MOMENTUM * moment + gradient
    weight_new = weight - step_rate * (gradient + MOMENTUM * moment_new)
    average_new = AVERAGING * average + (1.0 - AVERAGING) * weight_new
    return (gradient, moment_new, average_new, weight_new)


def swap(tensor, bit):
    count = lax.axis_size("dp")
    return lax.ppermute(tensor, "dp", [(i, i ^ bit) for i in range(count)])


def across_heads(tensor, bit):
    count = lax.axis_size("mp")
    return lax.ppermute(tensor, "mp", [(i, i ^ bit) for i in range(count)])


def bit_orders():
    bits = []
    while 2 ** len(bits) < lax.axis_size("dp"):
        bits.append(2 ** len(bits))
    outer = bits[1:]
    return (outer + bits[:1], outer[::-1] + bits[:1])


def split_three(tensor):
    high = lax.reduce_precision(tensor, 8, 7)
    rest = tensor - high
    middle = lax.reduce_precision(rest, 8, 7)
    return [high.astype(BF), middle.astype(BF), (rest - middle).astype(BF)]


def spread_on(pieces, order):
    held, offsets = jnp.concatenate(pieces, axis=0), [0, order[0]]
    for bit in order[1:-1]:
        held = jnp.concatenate([held, swap(held, bit)], axis=0)
        offsets = offsets + [k ^ bit for k in offsets]
    return [held, offsets]


def spread_out(group, order):
    held, offsets = group
    bit = order[-1]
    return [(held, offsets), (swap(held, bit), [k ^ bit for k in offsets])]


def spread_at_once(tensor, early):
    count = lax.axis_size("dp")
    groups = [list(range(side, count, 2)) for side in (0, 1)]
    copies = jnp.broadcast_to(tensor[None], (count // 2, *tensor.shape))
    held = lax.all_to_all(copies, "dp", 0, 0, axis_index_groups=groups, tiled=True)
    held = held.reshape(count // 2 * tensor.shape[0], tensor.shape[1])
    held, early = after(held, *early)
    return early, [
        (held, [(j, 0) for j in range(count // 2)]),
        (swap(held, 1), [(j, 1) for j in range(count // 2)]),
    ]


def spread_wide(pieces, own_sent, first_sent, order):
    offsets = [0, order[0], order[1], order[0] ^ order[1]]
    pieces = pieces + [own_sent, swap(first_sent, order[1])]
    for bit in order[2:-1]:
        pieces = pieces + [swap(piece, bit) for piece in pieces]
        offsets = offsets + [k ^ bit for k in offsets]
    return pieces, offsets


def spread_last(pieces, offsets, bit):
    pair = jnp.concatenate(pieces, axis=0)
    return [(pair, offsets), (swap(pair, bit), [k ^ bit for k in offsets])]


def round_up(number, unit):
    return -(-number // unit) * unit


def column_cuts(width):
    half = round_up(width // TILE, 2) // 2 * TILE
    first = round_up(half // TILE, 2) // 2 * TILE
    return half, [(0, first), (first, half), (half, width)]


def device_of(me, offset):
    if isinstance(offset, tuple):
        return 2 * offset[0] + ((me & 1) ^ offset[1])
    return me ^ offset


def lay(groups):
    share = groups[0][0].shape[0] // len(groups[0][1])
    if share % 16 == 0:
        return groups
    me = lax.axis_index("dp")
    count = lax.axis_size("dp")
    whole = jnp.zeros((count * share, groups[0][0].shape[1]), groups[0][0].dtype)
    for array, offsets in groups:
        for n, k in enumerate(offsets):
            part = array[n * share : (n + 1) * share]
            whole = lax.dynamic_update_slice(whole, part, (device_of(me, k) * share, 0))
    return [(whole, [])]


def arrays_of(groups):
    return [array for array, _ in groups]


def offsets_of(groups):
    return [offsets for _, offsets in groups]


def row_copies(me, shards, offsets, low, size, target, column, sem):
    copies = []
    columns, place = pl.ds(low, size), pl.ds(column, size)
    for shard, from_devices in zip(shards, offsets):
        if not from_devices:
            copies.append(
                pltpu.make_async_copy(shard.at[:, columns], target.at[:, place], sem)
            )
        for n, k in enumerate(from_devices):
            share = shard.shape[0] // len(from_devices)
            rows = pl.ds(pl.multiple_of(device_of(me, k) * share, 16), share)
            source = shard.at[pl.ds(n * share, share), columns]
            copies.append(pltpu.make_async_copy(source, target.at[rows, place], sem))
    return copies


def start_all(copies):
    for copy in copies:
        copy.start()


def wait_all(copies):
    for copy in copies:
        copy.wait()


def call(kernel, name, out_shape, operands, scratch):
    spaces = {
        "s": pl.BlockSpec(memory_space=pltpu.SMEM),
        "v": pl.BlockSpec(memory_space=pltpu.VMEM),
        "h": pl.BlockSpec(memory_space=pltpu.HBM),
    }
    return pl.pallas_call(
        kernel,
        out_shape=out_shape,
        in_specs=[spaces[space] for _, space in operands],
        out_specs=tuple(spaces["v"] for _ in out_shape),
        scratch_shapes=scratch,
        compiler_params=pltpu.CompilerParams(vmem_limit_bytes=VMEM_BYTES),
        cost_estimate=pl.CostEstimate(flops=1, transcendentals=0, bytes_accessed=1),
        name=name,
    )(*[array for array, _ in operands])


def shaped(rows, columns, kind=BF):
    return jax.ShapeDtypeStruct((rows, columns), kind)


def project(info, tokens, cosine, sine_tab, contexts):
    rows, width = tokens.shape
    own = rows // lax.axis_size("mp")
    block = min(rows, TILE)
    shards, offsets = arrays_of(contexts), offsets_of(contexts)
    wide = shards[0].shape[1]

    def kernel(info_ref, x_ref, cos_ref, sin_ref, *refs):
        shard_refs, refs = refs[: len(shards)], refs[len(shards) :]
        normed_ref, own_ref, key_ref, value_ref, gain_ref, w_c, sems = refs
        copies = row_copies(info_ref[0], shard_refs, offsets, 0, wide, w_c, 0, sems.at[0])
        start_all(copies)
        wait_all(copies)
        terms = w_c[:, 2 * HD : 2 * HD + LANES].astype(F32).T
        gains = terms[0:2] + terms[2:4] + terms[4:6]
        gain_ref[...] = jnp.concatenate([gains] * 4, axis=0)
        for r in range(0, rows, block):
            span = pl.ds(r, block)
            x = x_ref[span, :].astype(F32)
            normed = (x * inverse_rms(x) * gains[0:1]).astype(BF)
            normed_ref[span, :] = normed
            raw = mm(normed, w_c[:, : 2 * HD], ((1,), (0,)))
            key_ref[span, :] = rotate(raw[:, :HD], cos_ref[span, :], sin_ref[span, :]).astype(BF)
            value_ref[span, :] = raw[:, HD:].astype(BF)
        own_ref[...] = normed_ref[pl.ds(pl.multiple_of(info_ref[1], own), own), :]

    return call(
        kernel,
        "project",
        (
            shaped(rows, width),
            shaped(own, width),
            *[shaped(rows, HD)] * 2,
            shaped(8, width, F32),
        ),
        [(info, "s"), (tokens, "v"), (cosine, "v"), (sine_tab, "v")]
        + [(shard, "h") for shard in shards],
        [pltpu.VMEM((width, wide), BF), pltpu.SemaphoreType.DMA((1,))],
    )


def masked_scores(info_ref, query, keys):
    scores = mm(query, keys, ((1,), (1,))) * 0.0625
    at_row = info_ref[1] + lax.broadcasted_iota(jnp.int32, scores.shape, 0)
    at_key = lax.broadcasted_iota(jnp.int32, scores.shape, 1)
    allowed = (at_key <= at_row) & (at_key < info_ref[2])
    return jnp.where(allowed, scores, -1e30)


def attend(info, normed_own, keys, values, tokens_own, tables, gains, w_queries, w_outputs):
    own, width = tokens_own.shape
    q_shards, q_offsets = arrays_of(w_queries), offsets_of(w_queries)
    o_shards, o_offsets = arrays_of(w_outputs), offsets_of(w_outputs)
    across = q_shards[0].shape[1]

    def kernel(info_ref, own_ref, key_ref, value_ref, x_ref, cos_ref, sin_ref, gain_ref, *refs):
        q_refs, refs = refs[: len(q_shards)], refs[len(q_shards) :]
        o_refs, refs = refs[: len(o_shards)], refs[len(o_shards) :]
        query_ref, mixed_ref, middle_ref, normed_ref, log_ref, w_q, w_o, sems = refs
        copies = row_copies(info_ref[0], q_refs, q_offsets, 0, across, w_q, 0, sems.at[0])
        copies_o = row_copies(info_ref[0], o_refs, o_offsets, 0, across, w_o, 0, sems.at[1])
        start_all(copies)
        start_all(copies_o)
        wait_all(copies)
        keys, values = key_ref[...], value_ref[...]
        raw = mm(own_ref[...], w_q[...], ((1,), (0,)))
        for h in range(across // HD):
            columns = slice(h * HD, (h + 1) * HD)
            query = rotate(raw[:, columns], cos_ref[...], sin_ref[...]).astype(BF)
            query_ref[:, columns] = query
            scores = masked_scores(info_ref, query, keys)
            highest = jnp.max(scores, axis=-1, keepdims=True)
            exped = jnp.exp(scores - highest)
            total = jnp.sum(exped, axis=-1, keepdims=True)
            probs = (exped * (1.0 / total)).astype(BF)
            mixed_ref[:, columns] = mm(probs, values, ((1,), (0,))).astype(BF)
            log_ref[:, h : h + 1] = highest + jnp.log(total)
        wait_all(copies_o)
        middle = x_ref[...].astype(F32) + mm(mixed_ref[...], w_o[...], ((1,), (1,)))
        middle_ref[...] = middle
        normed_ref[...] = (middle * inverse_rms(middle) * gain_ref[1:2, :]).astype(BF)

    return call(
        kernel,
        "attend",
        (
            shaped(own, across),
            shaped(own, across),
            shaped(own, width, F32),
            shaped(own, width),
            shaped(own, LANES, F32),
        ),
        [(info, "s")]
        + [(array, "v") for array in (normed_own, keys, values, tokens_own, *tables, gains)]
        + [(shard, "h") for shard in q_shards + o_shards],
        [pltpu.VMEM((width, across), BF)] * 2 + [pltpu.SemaphoreType.DMA((2,))],
    )


def attend_back(
    info, parts, middle, grad_own, gains, queries, keys, values, log_sums, tables, w_outputs
):
    heads, n_parts = queries.shape[1] // HD, len(parts)
    own, width = middle.shape
    rows = keys.shape[0]
    output_shards, offsets = arrays_of(w_outputs), offsets_of(w_outputs)
    count = len(output_shards)

    def kernel(info_ref, *refs):
        part_refs, refs = refs[:n_parts], refs[n_parts:]
        middle_ref, grad_ref, gain_ref = refs[:3]
        query_ref, refs = refs[3], refs[4:]
        key_ref, value_ref, log_ref, cos_ref, sin_ref, cos_own, sin_own = refs[:7]
        shards, refs = refs[7 : 7 + count], refs[7 + count :]
        grad_middle_ref, low_ref, gain_two_ref, query_out, context_out, w_o, sem = refs
        copies = row_copies(info_ref[0], shards, offsets, 0, heads * HD, w_o, 0, sem.at[0])
        start_all(copies)
        grad_in = part_refs[0][...]
        for part_ref in part_refs[1:]:
            grad_in = grad_in + part_ref[...].astype(F32)
        middle = middle_ref[...]
        inverse = inverse_rms(middle)
        unit = middle * inverse
        gain_two = jnp.sum(grad_in * unit, axis=0, keepdims=True)
        gain_two_ref[...] = jnp.broadcast_to(gain_two, gain_two_ref.shape)
        grad_middle = grad_ref[...].astype(F32) + norm_back(
            grad_in, unit, inverse, gain_ref[1:2, :]
        )
        grad_middle_ref[...] = grad_middle
        low = grad_middle.astype(BF)
        low_ref[...] = low
        wait_all(copies)
        keys, values = key_ref[...], value_ref[...]
        grad_mixed = mm(low, w_o[...], ((1,), (0,))).astype(BF)
        grad_keys = grad_values = None
        for h in range(heads):
            query = query_ref[:, h * HD : (h + 1) * HD]
            scores = masked_scores(info_ref, query, keys)
            probs = jnp.exp(scores - log_ref[:, h : h + 1])
            grad_head = grad_mixed[:, h * HD : (h + 1) * HD]
            grad_probs = mm(grad_head, values, ((1,), (1,)))
            inner = jnp.sum(probs * grad_probs, axis=-1, keepdims=True)
            grad_scores = (probs * (grad_probs - inner)).astype(BF)
            turned = mm(grad_scores, keys, ((1,), (0,))) * 0.0625
            query_out[:, h * HD : (h + 1) * HD] = rotate(
                turned, cos_own[...], -sin_own[...]
            ).astype(BF)
            term_keys = mm(grad_scores, query, ((0,), (0,)))
            term_values = mm(probs.astype(BF), grad_head, ((0,), (0,)))
            grad_keys = term_keys if h == 0 else grad_keys + term_keys
            grad_values = term_values if h == 0 else grad_values + term_values
        context_out[:, :HD] = rotate(grad_keys * 0.0625, cos_ref[...], -sin_ref[...]).astype(BF)
        context_out[:, HD:] = grad_values.astype(BF)

    return call(
        kernel,
        "attend_back",
        (
            shaped(own, width, F32),
            shaped(own, width),
            shaped(8, width, F32),
            shaped(own, heads * HD),
            shaped(rows, 2 * HD),
        ),
        [(info, "s")]
        + [(part, "v") for part in parts]
        + [(middle, "v"), (grad_own, "v"), (gains, "v"), (queries, "v")]
        + [(array, "v") for array in (keys, values, log_sums, *tables)]
        + [(shard, "h") for shard in output_shards],
        [pltpu.VMEM((width, heads * HD), BF), pltpu.SemaphoreType.DMA((1,))],
    )


def store_sides(side, value, made, column, keep_ref, send_ref):
    blocks, share, _ = keep_ref.shape
    size = value.shape[1]
    for b in range(2 * blocks):
        made[b // 2, b % 2, :, :size] = value[b * share : (b + 1) * share].astype(BF)
    for b in range(blocks):
        keep_ref[b, :, column : column + size] = made[b, side, :, :size]
        send_ref[b, :, column : column + size] = made[b, 1 - side, :, :size]


def mixer_grads(
    info, normed, normed_own, grad_query, grad_context, low, mixed, gain_two, w_shards
):
    query_shards, context_shards = (arrays_of(groups) for groups in w_shards)
    offsets_q, offsets_c = (offsets_of(groups) for groups in w_shards)
    width = normed.shape[1]
    dp = lax.axis_size("dp")
    share = width // dp
    across = grad_query.shape[1]
    count = len(query_shards)
    first = jax.ShapeDtypeStruct((dp // 2, share, across + HD + LANES), BF)
    second = jax.ShapeDtypeStruct((dp // 2, share, across + HD), BF)

    def kernel(info_ref, *refs):
        normed_ref, own_ref, query_ref, context_ref, low_ref, mixed_ref, gain_ref = refs[:7]
        queries, contexts = refs[7 : 7 + count], refs[7 + count : 7 + 2 * count]
        keep_a, send_a, keep_b, send_b, w_q, w_c, made, sems = refs[7 + 2 * count :]
        side = info_ref[3]
        copies = row_copies(info_ref[0], queries, offsets_q, 0, across, w_q, 0, sems.at[0])
        copies_c = row_copies(info_ref[0], contexts, offsets_c, 0, 2 * HD, w_c, 0, sems.at[1])
        start_all(copies)
        start_all(copies_c)
        d_output = mm(low_ref[...], mixed_ref[...], ((0,), (0,)))
        halfway = across // HD // 2
        for h in range(across // HD):
            keep, send = (keep_a, send_a) if h < halfway else (keep_b, send_b)
            at = (2 * (h % halfway) + 1) * HD
            store_sides(side, d_output[:, h * HD : (h + 1) * HD], made, at, keep, send)
        d_query = mm(own_ref[...], query_ref[...], ((0,), (0,)))
        for h in range(across // HD):
            keep, send = (keep_a, send_a) if h < halfway else (keep_b, send_b)
            at = 2 * (h % halfway) * HD
            store_sides(side, d_query[:, h * HD : (h + 1) * HD], made, at, keep, send)
        d_context = mm(normed_ref[...], context_ref[...], ((0,), (0,)))
        store_sides(side, d_context[:, :HD], made, across, keep_a, send_a)
        store_sides(side, d_context[:, HD:], made, across, keep_b, send_b)
        wait_all(copies)
        wait_all(copies_c)
        gain_one = jnp.sum(d_query * w_q[...].astype(F32), axis=1, keepdims=True) + jnp.sum(
            d_context * w_c[...].astype(F32), axis=1, keepdims=True
        )
        second_gain = gain_ref[...].T
        lane = lax.broadcasted_iota(jnp.int32, (width, LANES), 1)
        both = jnp.where(lane == 0, gain_one, jnp.where(lane == 1, second_gain[:, 0:1], 0.0))
        store_sides(side, both, made, across + HD, keep_a, send_a)

    return call(
        kernel,
        "mixer_grads",
        (first, first, second, second),
        [(info, "s")]
        + [
            (array, "v")
            for array in (normed, normed_own, grad_query, grad_context, low, mixed, gain_two)
        ]
        + [(shard, "h") for shard in query_shards + context_shards],
        [
            pltpu.VMEM((width, across), BF),
            pltpu.VMEM((width, 2 * HD), BF),
            pltpu.VMEM((dp // 2, 2, share, across), BF),
            pltpu.SemaphoreType.DMA((2,)),
        ],
    )


def finish(info, grad_query, parts, grad_middle, tokens_own, gains, w_shards):
    query_shards, context_shards = (arrays_of(groups) for groups in w_shards)
    offsets_q, offsets_c = (offsets_of(groups) for groups in w_shards)
    own, width = grad_middle.shape
    across = grad_query.shape[1]
    count, n_parts = len(query_shards), len(parts)

    def kernel(info_ref, query_ref, *refs):
        part_refs, refs = refs[:n_parts], refs[n_parts:]
        middle_ref, x_ref, gain_ref = refs[:3]
        queries, contexts = refs[3 : 3 + count], refs[3 + count : 3 + 2 * count]
        out_ref, w_q, w_c, sems = refs[3 + 2 * count :]
        copies = row_copies(info_ref[0], queries, offsets_q, 0, across, w_q, 0, sems.at[0])
        copies_c = row_copies(info_ref[0], contexts, offsets_c, 0, 2 * HD, w_c, 0, sems.at[1])
        start_all(copies)
        start_all(copies_c)
        total = part_refs[0][...].astype(F32)
        for part_ref in part_refs[1:]:
            total = total + part_ref[...].astype(F32)
        x = x_ref[...].astype(F32)
        inverse = inverse_rms(x)
        wait_all(copies)
        wait_all(copies_c)
        grad_in = mm(query_ref[...], w_q[...], ((1,), (1,))) + mm(
            total.astype(BF), w_c[...], ((1,), (1,))
        )
        out_ref[...] = middle_ref[...] + norm_back(grad_in, x * inverse, inverse, gain_ref[0:1, :])

    return call(
        kernel,
        "finish",
        (shaped(own, width, F32),),
        [(info, "s"), (grad_query, "v")]
        + [(part, "v") for part in parts]
        + [(grad_middle, "v"), (tokens_own, "v"), (gains, "v")]
        + [(shard, "h") for shard in query_shards + context_shards],
        [
            pltpu.VMEM((width, across), BF),
            pltpu.VMEM((width, 2 * HD), BF),
            pltpu.SemaphoreType.DMA((2,)),
        ],
    )[0]


def feed_block(info, x, g, groups_a, groups_b, width, out_type):
    rows, depth = x.shape
    shards_a, shards_b = arrays_of(groups_a), arrays_of(groups_b)
    offsets, offsets_b = offsets_of(groups_a), offsets_of(groups_b)
    count = len(shards_a)
    half, cuts = column_cuts(width)

    def kernel(info_ref, x_ref, g_ref, *refs):
        first, second = refs[:count], refs[count : 2 * count]
        hid_ref, gate_ref, up_ref, feed_ref, back_ref = refs[2 * count : 2 * count + 5]
        w_gate, w_up, w_down, sems = refs[2 * count + 5 :]
        copies = []
        for n, (low, high) in enumerate(cuts):
            size = high - low
            source, at = (first, width + low) if high <= half else (second, width + low - half)
            group = []
            for shards, start, target in (
                (first, low, w_gate),
                (second, low, w_up),
                (source, at, w_down),
            ):
                own_offsets = offsets_b if shards is second else offsets
                group += row_copies(
                    info_ref[0], shards, own_offsets, start, size, target, low, sems.at[n]
                )
            copies.append(group)
            start_all(group)
        scale = 0.7978845608028654
        feed = back = None
        for n, (low, high) in enumerate(cuts):
            wait_all(copies[n])
            x, g = x_ref[...], g_ref[...]
            gate_w, up_w, down_w = w_gate[:, low:high], w_up[:, low:high], w_down[:, low:high]
            gate = mm(x, gate_w, ((1,), (0,)))
            up = mm(x, up_w, ((1,), (0,)))
            grad = mm(g, down_w, ((1,), (0,)))
            square = gate * gate
            tanh = jnp.tanh(scale * gate * (1.0 + 0.044715 * square))
            right = 0.5 * (1.0 + tanh)
            gelu = gate * right
            slope = right + gelu * (1.0 - tanh) * scale * (1.0 + 3 * 0.044715 * square)
            hidden = (gelu * up).astype(BF)
            grad_gate = (grad * up * slope).astype(BF)
            grad_up = (grad * gelu).astype(BF)
            hid_ref[:, low:high] = hidden
            gate_ref[:, low:high] = grad_gate
            up_ref[:, low:high] = grad_up
            feed_n = mm(hidden, down_w, ((1,), (1,)))
            back_n = mm(grad_gate, gate_w, ((1,), (1,))) + mm(grad_up, up_w, ((1,), (1,)))
            feed = feed_n if feed is None else feed + feed_n
            back = back_n if back is None else back + back_n
        feed_ref[...] = feed.astype(feed_ref.dtype)
        back_ref[...] = back.astype(back_ref.dtype)

    return call(
        kernel,
        "feed_block",
        (*[shaped(rows, width)] * 3, *[shaped(rows, depth, out_type)] * 2),
        [(info, "s"), (x, "v"), (g, "v")] + [(shard, "h") for shard in shards_a + shards_b],
        [pltpu.VMEM((depth, width), BF)] * 3 + [pltpu.SemaphoreType.DMA((3,))],
    )


def feed_grads(info, lefts, rights, low, high, firsts, whole):
    parts, dp = len(lefts), lax.axis_size("dp")
    depth, width = lefts[0].shape
    share = width // dp
    full = whole[0].shape[1]
    n_whole, n_part = full // TILE, (high - low) // TILE
    half = jax.ShapeDtypeStruct((dp // 2, share, full + high - low), BF)

    def kernel(info_ref, *refs):
        first_refs, whole_refs = refs[:parts], refs[parts : 2 * parts]
        left_refs, right_refs = refs[2 * parts : 3 * parts], refs[3 * parts : 4 * parts]
        keep_ref, send_ref, made = refs[4 * parts :]

        def one(rows, columns):
            total = None
            for row, column in zip(rows, columns):
                term = mm(row[...], column[...], ((0,), (0,)))
                total = term if total is None else total + term
            store_sides(info_ref[3], total, made, 0, keep_ref, send_ref)

        @pl.when(pl.program_id(0) < n_whole)
        def _():
            one(first_refs, whole_refs)

        @pl.when(pl.program_id(0) >= n_whole)
        def _():
            one(left_refs, right_refs)

    def whole_map(f, info_ref):
        return (0, jnp.minimum(f, n_whole - 1))

    def part_map(f, info_ref):
        return (0, low // TILE + jnp.maximum(f - n_whole, 0))

    fixed = pl.BlockSpec((depth, width), lambda f, info_ref: (0, 0))
    return pl.pallas_call(
        kernel,
        out_shape=(half, half),
        grid_spec=pltpu.PrefetchScalarGridSpec(
            num_scalar_prefetch=1,
            grid=(n_whole + n_part,),
            in_specs=[fixed] * parts
            + [pl.BlockSpec((depth, TILE), whole_map)] * parts
            + [fixed] * parts
            + [pl.BlockSpec((depth, TILE), part_map)] * parts,
            out_specs=[pl.BlockSpec((dp // 2, share, TILE), lambda f, info_ref: (0, 0, f))] * 2,
            scratch_shapes=[pltpu.VMEM((dp // 2, 2, share, TILE), BF)],
        ),
        compiler_params=pltpu.CompilerParams(vmem_limit_bytes=VMEM_BYTES),
        cost_estimate=pl.CostEstimate(flops=1, transcendentals=0, bytes_accessed=1),
        name="feed_grads",
    )(info, *firsts, *whole, *lefts, *rights)


class Halving:
    def __init__(self, keep, send, order):
        self.order = order
        self.left = [2**j for j in reversed(range(len(order)))]
        self.sent = swap(send, order[0])
        self.kept = keep
        self.left.remove(order[0])
        self.stage = 1

    def halve(self):
        me = lax.axis_index("dp")
        total = (self.kept.astype(F32) + self.sent.astype(F32)).astype(BF)
        bit = self.order[self.stage]
        total = total.reshape((2,) * len(self.left) + total.shape[-2:])
        axis = self.left.index(bit)
        side = (me // bit) % 2
        self.kept = lax.dynamic_index_in_dim(total, side, axis, keepdims=False)
        self.ready = lax.dynamic_index_in_dim(total, 1 - side, axis, keepdims=False)
        self.left.remove(bit)

    def send(self):
        self.sent = swap(self.ready, self.order[self.stage])
        self.stage += 1

    def step(self):
        self.halve()
        self.send()

    def done(self):
        while self.stage < len(self.order):
            self.step()
        return self.kept.astype(F32) + self.sent.astype(F32)


def step_both(first, second):
    first.halve()
    second.halve()
    first.kept, (second.kept, first.ready, second.ready) = after(
        first.kept, second.kept, first.ready, second.ready
    )
    first.send()
    second.send()


def after(values, *others):
    flat, tree = jax.tree.flatten((values, others))
    return jax.tree.unflatten(tree, lax.optimization_barrier(flat))


def local(
    tokens,
    cotangent,
    lengths,
    rates,
    query_weight,
    query_moment,
    query_average,
    output_weight,
    output_moment,
    output_average,
    gating_weight,
    gating_moment,
    gating_average,
    down_weight,
    down_moment,
    down_average,
    context_weight,
    context_moment,
    context_average,
    gains_weight,
    gains_moment,
    gains_average,
):
    row_count, width = tokens.shape
    dp, mp = lax.axis_size("dp"), lax.axis_size("mp")
    place = lax.axis_index("mp")
    own_count = row_count // mp
    own_start = place * own_count
    share, piece = width // dp, width // (dp * mp)
    forth, back = bit_orders()
    forth_first, back_first = forth[-1:] + forth[:-1], back[-1:] + back[:-1]
    length = lengths[0]
    places = jnp.arange(row_count, dtype=jnp.int32)
    me = lax.axis_index("dp")
    info = jnp.stack([me, own_start, length, me % 2]).astype(jnp.int32)

    def rows_at(tensor, step, count):
        return lax.dynamic_slice_in_dim(tensor, (place ^ step) * count, count, 0)

    gains_split = jnp.stack(split_three(gains_weight)).reshape(1, -1)
    message = jnp.concatenate(
        [
            query_weight.astype(BF),
            output_weight.T.astype(BF),
            context_weight.astype(BF).reshape(2 * piece, HD),
            jnp.pad(gains_split, ((0, 0), (0, HD - gains_split.shape[1]))),
        ],
        axis=0,
    )
    message = jnp.pad(message, ((0, -message.shape[0] % 16), (0, 0)))
    copies = jnp.broadcast_to(message[None], (mp, *message.shape))
    line = lax.all_to_all(copies, "mp", 0, 0, tiled=True)
    parts = [lax.dynamic_index_in_dim(line, place ^ k, 0, keepdims=False) for k in range(mp)]
    query_share = jnp.concatenate([part[:share] for part in parts], axis=1)
    output_share = jnp.concatenate([part[share : 2 * share] for part in parts], axis=1)
    rests = [line[k, 2 * share :] for k in range(mp)]
    context_share = jnp.concatenate(
        [
            jnp.concatenate(
                [
                    rest[:piece],
                    rest[piece : 2 * piece],
                    jnp.pad(
                        rest[2 * piece, : 6 * piece].reshape(6, piece).T, ((0, 0), (0, LANES - 6))
                    ),
                ],
                axis=1,
            )
            for rest in rests
        ],
        axis=0,
    )

    units = gating_weight.shape[2]
    padded = round_up(units, TILE)
    half = column_cuts(padded)[0]

    def pad_units(tensor):
        return jnp.pad(tensor, ((0, 0), (0, padded - units)))

    gating_low = gating_weight.astype(BF)
    down_low = pad_units(down_weight.T.astype(BF))
    feed_a = jnp.concatenate([pad_units(gating_low[0]), down_low[:, :half]], axis=1)
    feed_b = jnp.concatenate([pad_units(gating_low[1]), down_low[:, half:]], axis=1)
    first_a, first_b = swap(feed_a, forth[0]), swap(feed_b, back[0])
    own_a, own_b = swap(feed_a, forth[1]), swap(feed_b, back[1])
    early, contexts = spread_at_once(context_share, (first_a, first_b, own_a, own_b))
    first_a, first_b, own_a, own_b = early
    held_q, held_o = [query_share, swap(query_share, forth[0])], [output_share, swap(output_share, back[0])]

    cosine, sine_tab = rotation(row_count, HD)
    tokens_own = rows_at(tokens, 0, own_count)
    tables_own = (rows_at(cosine, 0, own_count), rows_at(sine_tab, 0, own_count))
    context_near, (tokens_own, tables_own) = after(contexts[1][0], tokens_own, tables_own)
    contexts = [contexts[0], (context_near, contexts[1][1])]
    contexts = lay(contexts)
    normed, normed_own, keys, values, gains = project(info, tokens, cosine, sine_tab, contexts)
    (held_q, held_o, cotangent_too), (gains,) = after((held_q, held_o, cotangent), gains)
    grad_low = jnp.where((places < length)[:, None], cotangent_too, jnp.zeros_like(cotangent))
    grad_blocks = [rows_at(grad_low, k, own_count) for k in range(mp)]
    w_queries = spread_on(held_q, forth)
    w_outputs = spread_on(held_o, back)
    w_queries[0], (grad_blocks,) = after(w_queries[0], grad_blocks)
    (sent_a, sent_b), (w_queries[0], w_outputs[0]) = after(
        (first_a, first_b), w_queries[0], w_outputs[0]
    )
    w_queries, w_outputs = spread_out(w_queries, forth), spread_out(w_outputs, back)
    w_queries, w_outputs = lay(w_queries), lay(w_outputs)
    pieces_a, offsets_a = spread_wide([feed_a, first_a], own_a, sent_a, forth)
    pieces_b, offsets_b = spread_wide([feed_b, first_b], own_b, sent_b, back)
    shards_a = spread_last(pieces_a[:2], offsets_a[:2], forth[-1])
    shards_b = spread_last(pieces_b[:2], offsets_b[:2], back[-1])
    normed_own, (shards_a, shards_b, grad_blocks) = after(
        normed_own, arrays_of(shards_a), arrays_of(shards_b), grad_blocks
    )
    shards_a = list(zip(shards_a, [offsets_a[:2], [k ^ 1 for k in offsets_a[:2]]]))
    shards_b = list(zip(shards_b, [offsets_b[:2], [k ^ 1 for k in offsets_b[:2]]]))
    queries, mixed, middle, normed_two_own, log_sums = attend(
        info, normed_own, keys, values, tokens_own, tables_own, gains, w_queries, w_outputs
    )

    (pieces_a[2:], pieces_b[2:]), (normed_two_own,) = after(
        (pieces_a[2:], pieces_b[2:]), normed_two_own
    )
    for n in range(2, len(pieces_a), 2):
        shards_a = shards_a + spread_last(pieces_a[n : n + 2], offsets_a[n : n + 2], forth[-1])
        shards_b = shards_b + spread_last(pieces_b[n : n + 2], offsets_b[n : n + 2], back[-1])
    shards_a, shards_b = lay(shards_a), lay(shards_b)
    blocks = [normed_two_own] + [across_heads(normed_two_own, k) for k in range(1, mp)]
    made = []
    for k in range(mp):
        if k > 0:
            blocks[k], (made[k - 1],) = after(blocks[k], made[k - 1])
        made.append(
            feed_block(
                info, blocks[k], grad_blocks[k], shards_a, shards_b, padded, F32 if k == 0 else BF
            )
        )
    hidden, grad_gate, grad_up, feed_parts, back_parts = (
        [made[k][n] for k in range(mp)] for n in range(5)
    )
    back_parts = back_parts[:1] + [across_heads(back_parts[k], k) for k in range(1, mp)]
    grad_up, (back_parts[1],) = after(grad_up, back_parts[1])
    keep_b, send_b = feed_grads(info, grad_blocks, hidden, half, padded, blocks, grad_up)
    grad_gate, (keep_b, back_parts[2:-1]) = after(grad_gate, keep_b, back_parts[2:-1])
    keep_a, send_a = feed_grads(info, grad_blocks, hidden, 0, half, blocks, grad_gate)
    held = (back_parts, feed_parts, keep_a, keep_b, normed, normed_own, mixed, middle, queries)
    held += (keys, values, log_sums, gains, cosine, sine_tab, tables_own, tokens_own, grad_blocks)
    held += (arrays_of(w_queries), arrays_of(contexts), arrays_of(w_outputs))
    (send_a, send_b), held = after((send_a, send_b), *held)
    back_parts, feed_parts, keep_a, keep_b, normed, normed_own, mixed, middle, queries = held[:9]
    keys, values, log_sums, gains, cosine, sine_tab, tables_own, tokens_own, grad_blocks = held[9:18]
    w_queries = list(zip(held[18], offsets_of(w_queries)))
    contexts = list(zip(held[19], offsets_of(contexts)))
    w_outputs = list(zip(held[20], offsets_of(w_outputs)))
    flow_a, flow_b = Halving(keep_a, send_a, forth_first), Halving(keep_b, send_b, back_first)
    flow_a.sent, (flow_b.sent, flow_a.kept, flow_b.kept) = after(
        flow_a.sent, flow_b.sent, flow_a.kept, flow_b.kept
    )
    step_both(flow_a, flow_b)
    feed_parts, (back_parts,) = after(feed_parts, back_parts)
    feed_line = jnp.stack([part.astype(BF) for part in feed_parts])
    feed_line = jnp.stack(
        [lax.dynamic_index_in_dim(feed_line, place ^ k, 0, keepdims=False) for k in range(mp)]
    )
    feed_line = lax.all_to_all(feed_line, "mp", 0, 0, tiled=True)
    back_parts, (flow_a.kept, flow_b.kept) = after(back_parts, flow_a.kept, flow_b.kept)

    grad_middle, middle_low, gain_two, grad_query, grad_context = attend_back(
        info,
        back_parts,
        middle,
        grad_blocks[0],
        gains,
        queries,
        keys,
        values,
        log_sums,
        (cosine, sine_tab, *tables_own),
        w_outputs,
    )

    w_shards = (w_queries, contexts)
    keep_a, send_a, keep_b, send_b = mixer_grads(
        info, normed, normed_own, grad_query, grad_context, middle_low, mixed, gain_two, w_shards
    )
    (send_a, send_b), (flow_a.sent, flow_b.sent) = after((send_a, send_b), flow_a.sent, flow_b.sent)
    step_both(flow_a, flow_b)
    mixer_a, mixer_b = Halving(keep_a, send_a, forth_first), Halving(keep_b, send_b, back_first)
    mixer_a.sent, (mixer_b.sent, flow_a.kept, flow_b.kept) = after(
        mixer_a.sent, mixer_b.sent, flow_a.kept, flow_b.kept
    )
    step_both(mixer_a, mixer_b)
    mixer_a.sent, (mixer_b.sent, mixer_a.kept, mixer_b.kept, flow_a.sent, flow_b.sent) = after(
        mixer_a.sent, mixer_b.sent, mixer_a.kept, mixer_b.kept, flow_a.sent, flow_b.sent
    )
    step_both(mixer_a, mixer_b)
    (flow_a.sent, flow_b.sent), (mixer_a.sent, mixer_b.sent) = after(
        (flow_a.sent, flow_b.sent), mixer_a.sent, mixer_b.sent
    )
    context_line, (feed_line,) = after(grad_context, feed_line)
    context_line = context_line.reshape(mp, own_count, 2 * HD)
    context_line = lax.all_to_all(context_line, "mp", 0, 0, tiled=True)
    feed_one, feed_two = flow_a.done(), flow_b.done()
    mixer_one, mixer_two = mixer_a.done(), mixer_b.done()
    across, halfway = grad_query.shape[1], mp // 2
    shares = [
        (mixer_one if k < halfway else mixer_two)[
            :, (k % halfway) * 2 * HD : (k % halfway + 1) * 2 * HD
        ]
        for k in range(mp)
    ]
    share_context = jnp.concatenate([mixer_one[:, across:], mixer_two[:, across:]], axis=1)
    wide = share_context.shape[1]
    total = shares[0]
    for k in range(1, mp):
        total = total + across_heads(shares[k].astype(BF), k).astype(F32)
    sum_context = rows_at(share_context, 0, piece)
    for k in range(1, mp):
        sent = across_heads(rows_at(share_context, k, piece).astype(BF), k)
        sum_context = sum_context + sent.astype(F32)
    context_own = jnp.sum(context_line.astype(F32), axis=0)
    tokens_grad = finish(info, grad_query, [context_own], grad_middle, tokens_own, gains, w_shards)
    block_out = middle + jnp.sum(feed_line.astype(F32), axis=0)

    total, (tokens_grad,) = after(total, tokens_grad)
    sum_query, sum_output = total[:, :HD], total[:, HD:].T
    sum_gains = jnp.stack([sum_context[:, HD] / gains_weight[0], sum_context[:, HD + 1]])
    sum_context = jnp.stack([sum_context[:, :HD], sum_context[:, wide - HD :]])
    sum_gating = jnp.stack([feed_one[:, :units], feed_two[:, :units]])
    sum_down = jnp.concatenate([feed_one[:, padded:], feed_two[:, padded:]], axis=1)[:, :units].T

    query_grads, query_moments, query_averages, query_updated = advance(
        sum_query, query_moment, query_average, query_weight, rates[0]
    )
    output_grads, output_moments, output_averages, output_updated = advance(
        sum_output, output_moment, output_average, output_weight, rates[1]
    )
    gating_grads, gating_moments, gating_averages, gating_updated = advance(
        sum_gating, gating_moment, gating_average, gating_weight, rates[2]
    )
    down_grads, down_moments, down_averages, down_updated = advance(
        sum_down, down_moment, down_average, down_weight, rates[3]
    )
    context_grads, context_moments, context_averages, context_updated = advance(
        sum_context, context_moment, context_average, context_weight, rates[4]
    )
    gains_grads, gains_moments, gains_averages, gains_updated = advance(
        sum_gains, gains_moment, gains_average, gains_weight, rates[5]
    )
    return (
        block_out,
        tokens_grad,
        query_grads,
        query_moments,
        query_averages,
        query_updated,
        output_grads,
        output_moments,
        output_averages,
        output_updated,
        gating_grads,
        gating_moments,
        gating_averages,
        gating_updated,
        down_grads,
        down_moments,
        down_averages,
        down_updated,
        context_grads,
        context_moments,
        context_averages,
        context_updated,
        gains_grads,
        gains_moments,
        gains_averages,
        gains_updated,
    )


def solution(mesh):
    return jax.shard_map(
        local,
        mesh=mesh,
        in_specs=(
            P("dp", None),
            P("dp", None),
            P("dp"),
            P(),
            P("dp", "mp"),
            P("dp", "mp"),
            P("dp", "mp"),
            P("mp", "dp"),
            P("mp", "dp"),
            P("mp", "dp"),
            P(None, "dp", "mp"),
            P(None, "dp", "mp"),
            P(None, "dp", "mp"),
            P("mp", "dp"),
            P("mp", "dp"),
            P("mp", "dp"),
            P(None, ("dp", "mp"), None),
            P(None, ("dp", "mp"), None),
            P(None, ("dp", "mp"), None),
            P(None, ("dp", "mp")),
            P(None, ("dp", "mp")),
            P(None, ("dp", "mp")),
        ),
        out_specs=(
            P(("dp", "mp"), None),
            P(("dp", "mp"), None),
            P("dp", "mp"),
            P("dp", "mp"),
            P("dp", "mp"),
            P("dp", "mp"),
            P("mp", "dp"),
            P("mp", "dp"),
            P("mp", "dp"),
            P("mp", "dp"),
            P(None, "dp", "mp"),
            P(None, "dp", "mp"),
            P(None, "dp", "mp"),
            P(None, "dp", "mp"),
            P("mp", "dp"),
            P("mp", "dp"),
            P("mp", "dp"),
            P("mp", "dp"),
            P(None, ("dp", "mp"), None),
            P(None, ("dp", "mp"), None),
            P(None, ("dp", "mp"), None),
            P(None, ("dp", "mp"), None),
            P(None, ("dp", "mp")),
            P(None, ("dp", "mp")),
            P(None, ("dp", "mp")),
            P(None, ("dp", "mp")),
        ),
        check_vma=False,
    )
```

profile of v0, /device:TPU:0, one launch (start us, length us, event | category | flops | bytes accessed | tf_op | source)
XLA Modules:
  0.0 372.4 jit_solution(9339397816699042967)
XLA Ops:
  0.7 1.7 convert_element_type.219
  4.7 2.9 collective-permute-start
  10.4 4.9 %all-to-all-start = ((bf16[4,368,256]{2,1,0:T(8,128)(2,1)}), bf16[4,368,256]{2,1,0:T(8,128)(2,1)S(1)}, u32[]{:S(2)}, u32[]{:S(2)}) async-start(bf16[4,368,256]{2,1,0:T(8,128)(2,1)} %broadcast_in_dim.11), calls=%async_computation | async-start | bytes 1507328 | tf_op jit(solution)/shard_map/all_to_all | solution.py:717
  19.4 1.9 multiply_sine_fusion
  22.9 11.1 %all-to-all-done = bf16[4,368,256]{2,1,0:T(8,128)(2,1)S(1)} async-done(((bf16[4,368,256]{2,1,0:T(8,128)(2,1)}), bf16[4,368,256]{2,1,0:T(8,128)(2,1)S(1)}, u32[]{:S(2)}, u32[]{:S(2)}) %all-to-all-start) | async-done | bytes 753696 | tf_op jit(solution)/shard_map/all_to_all | solution.py:717
  36.0 3.8 %all-to-all-start.1 = ((bf16[4,144,640]{2,1,0:T(8,128)(2,1)}), bf16[4,144,640]{2,1,0:T(8,128)(2,1)S(1)}, u32[]{:S(2)}, u32[]{:S(2)}) async-start(bf16[4,144,640]{2,1,0:T(8,128)(2,1)} %broadcast_in_dim.12), calls=%async_computation.1 | async-start | bytes 1474560 | tf_op jit(solution)/shard_map/all_to_all | solution.py:98
  39.8 2.0 constant_dynamic-slice_fusion.10.x_ref.refs_2_
  42.5 2.0 collective-permute-start.4
  45.2 3.5 collective-permute-done.1
  50.2 2.3 all-to-all-done.1
  57.3 6.6 %project.1 = (bf16[1024,1152]{1,0:T(8,128)(2,1)}, bf16[256,1152]{1,0:T(8,128)(2,1)}, bf16[1024,256]{1,0:T(8,128)(2,1)}, bf16[1024,256]{1,0:T(8,128)(2,1)}, f32[8,1152]{1,0:T(8,128)}) custom-call(s32[4]{0:T(128)} %pad_add_fusion.info_ref, bf16[1024,1152]{1,0:T(8,128)(2,1)} %x_ref.1, f32[1024,128]{1,0:T(8,128)} %copy-done.19, f32[1024,128]{1,0:T(8,128)} %copy-done.18, ...), custom_call_target="tpu_custom_call" | custom-call | flops 1 | bytes 1 | tf_op jit(solution)/shard_map/project/pallas_call | solution.py:191
  65.2 1.6 collective-permute-start.7
  69.8 10.9 %collective-permute-done.7 = bf16[288,1024]{1,0:T(8,128)(2,1)S(1)} collective-permute-done((bf16[288,1024]{1,0:T(8,128)(2,1)S(1)}, bf16[288,1024]{1,0:T(8,128)(2,1)S(1)}, u32[]{:S(2)}, u32[]{:S(2)}) %collective-permute-start.7) | collective-permute-done | bytes 589856 | tf_op jit(solution)/shard_map/ppermute | solution.py:57
  89.9 8.6 %attend.1 = (bf16[256,1024]{1,0:T(8,128)(2,1)}, bf16[256,1024]{1,0:T(8,128)(2,1)}, f32[256,1152]{1,0:T(8,128)}, bf16[256,1152]{1,0:T(8,128)(2,1)}, f32[256,128]{1,0:T(8,128)}) custom-call(s32[4]{0:T(128)} %pad_add_fusion.info_ref, bf16[256,1152]{1,0:T(8,128)(2,1)} %get-tuple-element.372.own_ref.refs_1_, ...), custom_call_target="tpu_custom_call" | custom-call | flops 1 | bytes 1 | tf_op jit(solution)/shard_map/attend/pallas_call | solution.py:191
  98.6 5.4 %collective-permute-done.10 = bf16[144,2560]{1,0:T(8,128)(2,1)S(1)} collective-permute-done((bf16[144,2560]{1,0:T(8,128)(2,1)}, bf16[144,2560]{1,0:T(8,128)(2,1)S(1)}, u32[]{:S(2)}, u32[]{:S(2)}) %collective-permute-start.10) | collective-permute-done | bytes 737312 | tf_op jit(solution)/shard_map/ppermute | solution.py:57
  107.7 1.6 collective-permute-start.15
  109.2 2.6 collective-permute-start.18
  114.4 13.1 %feed_block.4 = (bf16[256,1792]{1,0:T(8,128)(2,1)}, bf16[256,1792]{1,0:T(8,128)(2,1)}, bf16[256,1792]{1,0:T(8,128)(2,1)}, f32[256,1152]{1,0:T(8,128)}, f32[256,1152]{1,0:T(8,128)}) custom-call(s32[4]{0:T(128)} %pad_add_fusion.info_ref, bf16[256,1152]{1,0:T(8,128)(2,1)} %get-tuple-element.255.x_ref.refs_0_, ...), custom_call_target="tpu_custom_call" | custom-call | flops 1 | bytes 1 | tf_op jit(solution)/shard_map/feed_block/pallas_call | solution.py:191
  127.6 6.7 %collective-permute-done.15.x_ref.refs_1_ = bf16[256,1152]{1,0:T(8,128)(2,1)S(1)} collective-permute-done((bf16[256,1152]{1,0:T(8,128)(2,1)S(1)}, bf16[256,1152]{1,0:T(8,128)(2,1)S(1)}, u32[]{:S(2)}, u32[]{:S(2)}) %collective-permute-start.15) | collective-permute-done | bytes 589856 | tf_op jit(solution)/shard_map/ppermute | solution.py:62
  135.1 12.5 %feed_block.5 = (bf16[256,1792]{1,0:T(8,128)(2,1)}, bf16[256,1792]{1,0:T(8,128)(2,1)}, bf16[256,1792]{1,0:T(8,128)(2,1)}, bf16[256,1152]{1,0:T(8,128)(2,1)}, bf16[256,1152]{1,0:T(8,128)(2,1)}) custom-call(s32[4]{0:T(128)} %pad_add_fusion.info_ref, bf16[256,1152]{1,0:T(8,128)(2,1)} %copy-done.21, bf16[256,1152]{1,0:T(8,128)(2,1)} %get-tuple-element.271.g_ref.refs_9_, ...), custom_call_target="tpu_custom_call" | custom-call | flops 1 | bytes 1 | tf_op jit(solution)/shard_map/feed_block/pallas_call | solution.py:191
  147.6 4.1 %collective-permute-done.18.x_ref.refs_2_ = bf16[256,1152]{1,0:T(8,128)(2,1)S(1)} collective-permute-done((bf16[256,1152]{1,0:T(8,128)(2,1)S(1)}, bf16[256,1152]{1,0:T(8,128)(2,1)S(1)}, u32[]{:S(2)}, u32[]{:S(2)}) %collective-permute-start.18) | collective-permute-done | bytes 589856 | tf_op jit(solution)/shard_map/ppermute | solution.py:62
  152.5 12.7 %feed_block.6 = (bf16[256,1792]{1,0:T(8,128)(2,1)}, bf16[256,1792]{1,0:T(8,128)(2,1)}, bf16[256,1792]{1,0:T(8,128)(2,1)}, bf16[256,1152]{1,0:T(8,128)(2,1)}, bf16[256,1152]{1,0:T(8,128)(2,1)}) custom-call(s32[4]{0:T(128)} %pad_add_fusion.info_ref, bf16[256,1152]{1,0:T(8,128)(2,1)} %copy-done.22, bf16[256,1152]{1,0:T(8,128)(2,1)} %get-tuple-element.278.g_ref.refs_10_, ...), custom_call_target="tpu_custom_call" | custom-call | flops 1 | bytes 1 | tf_op jit(solution)/shard_map/feed_block/pallas_call | solution.py:191
  165.2 2.3 collective-permute-start.21
  167.5 12.4 %feed_block.7 = (bf16[256,1792]{1,0:T(8,128)(2,1)}, bf16[256,1792]{1,0:T(8,128)(2,1)}, bf16[256,1792]{1,0:T(8,128)(2,1)}, bf16[256,1152]{1,0:T(8,128)(2,1)}, bf16[256,1152]{1,0:T(8,128)(2,1)}) custom-call(s32[4]{0:T(128)} %pad_add_fusion.info_ref, bf16[256,1152]{1,0:T(8,128)(2,1)} %collective-permute-done.19.x_ref.refs_3_, ...), custom_call_target="tpu_custom_call" | custom-call | flops 1 | bytes 1 | tf_op jit(solution)/shard_map/feed_block/pallas_call | solution.py:191
  181.3 15.3 %feed_grads.2 = (bf16[4,144,2560]{2,1,0:T(8,128)(2,1)}, bf16[4,144,2560]{2,1,0:T(8,128)(2,1)}) custom-call(s32[4]{0:T(128)} %pad_add_fusion.info_ref, bf16[256,1152]{1,0:T(8,128)(2,1)} %get-tuple-element.255.x_ref.refs_0_, bf16[256,1152]{1,0:T(8,128)(2,1)} %copy-done.21, bf16[256,1152]{1,0:T(8,128)(2,1)} %copy-done.22, ...), custom_call_target="tpu_custom_call" | custom-call | flops 1 | bytes 1 | tf_op jit(solution)/shard_map/feed_grads/pallas_call | solution.py:597
  196.7 6.3 %collective-permute-done.21.refs_2_ = bf16[256,1152]{1,0:T(8,128)(2,1)S(1)} collective-permute-done((bf16[256,1152]{1,0:T(8,128)(2,1)}, bf16[256,1152]{1,0:T(8,128)(2,1)S(1)}, u32[]{:S(2)}, u32[]{:S(2)}) %collective-permute-start.21) | collective-permute-done | bytes 589856 | tf_op jit(solution)/shard_map/ppermute | solution.py:62
  203.0 16.3 %feed_grads.3 = (bf16[4,144,2816]{2,1,0:T(8,128)(2,1)}, bf16[4,144,2816]{2,1,0:T(8,128)(2,1)}) custom-call(s32[4]{0:T(128)} %pad_add_fusion.info_ref, bf16[256,1152]{1,0:T(8,128)(2,1)} %get-tuple-element.255.x_ref.refs_0_, bf16[256,1152]{1,0:T(8,128)(2,1)} %copy-done.21, bf16[256,1152]{1,0:T(8,128)(2,1)} %copy-done.22, ...), custom_call_target="tpu_custom_call" | custom-call | flops 1 | bytes 1 | tf_op jit(solution)/shard_map/feed_grads/pallas_call | solution.py:597
  220.6 9.8 %collective-permute-done.24 = bf16[4,144,2560]{2,1,0:T(8,128)(2,1)} collective-permute-done((bf16[4,144,2560]{2,1,0:T(8,128)(2,1)}, bf16[4,144,2560]{2,1,0:T(8,128)(2,1)}, u32[]{:S(2)}, u32[]{:S(2)}) %collective-permute-start.24) | collective-permute-done | bytes 2949152 | tf_op jit(solution)/shard_map/ppermute | solution.py:57
  230.4 3.6 add_convert_fusion.1
  235.0 1.8 dynamic-slice_bitcast_fusion.2
  236.8 1.9 dynamic-slice_bitcast_fusion
  240.9 1.7 pad_maximum_fusion.1
  242.6 4.1 %all-to-all-start.2 = ((bf16[4,256,1152]{2,1,0:T(8,128)(2,1)}), bf16[4,256,1152]{2,1,0:T(8,128)(2,1)S(1)}, u32[]{:S(2)}, u32[]{:S(2)}) async-start(bf16[4,256,1152]{2,1,0:T(8,128)(2,1)} %pad_maximum_fusion.1), calls=%async_computation.2 | async-start | bytes 4718592 | tf_op jit(solution)/shard_map/all_to_all | solution.py:831
  246.7 11.0 %attend_back.1 = (f32[256,1152]{1,0:T(8,128)}, bf16[256,1152]{1,0:T(8,128)(2,1)}, f32[8,1152]{1,0:T(8,128)}, bf16[256,1024]{1,0:T(8,128)(2,1)}, bf16[1024,512]{1,0:T(8,128)(2,1)}) custom-call(s32[4]{0:T(128)} %pad_add_fusion.info_ref, f32[256,1152]{1,0:T(8,128)} %get-tuple-element.349.refs_0_, bf16[256,1152]{1,0:T(8,128)(2,1)} %copy-done.47, ...), custom_call_target="tpu_custom_call" | custom-call | flops 1 | bytes 1 | tf_op jit(solution)/shard_map/attend_back/pallas_call | solution.py:191
  257.7 9.7 %mixer_grads.1 = (bf16[4,144,1408]{2,1,0:T(8,128)(2,1)}, bf16[4,144,1408]{2,1,0:T(8,128)(2,1)}, bf16[4,144,1280]{2,1,0:T(8,128)(2,1)}, bf16[4,144,1280]{2,1,0:T(8,128)(2,1)}) custom-call(s32[4]{0:T(128)} %pad_add_fusion.info_ref, bf16[1024,1152]{1,0:T(8,128)(2,1)} %get-tuple-element.371.refs_0_, bf16[256,1152]{1,0:T(8,128)(2,1)} %get-tuple-element.372.own_ref.refs_1_, ...), custom_call_target="tpu_custom_call" | custom-call | flops 1 | bytes 1 | tf_op jit(solution)/shard_map/mixer_grads/pallas_call | solution.py:191
  267.4 6.2 %collective-permute-done.26 = bf16[2,144,2560]{2,1,0:T(8,128)(2,1)} collective-permute-done((bf16[2,144,2560]{2,1,0:T(8,128)(2,1)}, bf16[2,144,2560]{2,1,0:T(8,128)(2,1)}, u32[]{:S(2)}, u32[]{:S(2)}) %collective-permute-start.26) | collective-permute-done | bytes 1474592 | tf_op jit(solution)/shard_map/ppermute | solution.py:57
  273.6 2.9 collective-permute-done.25
  277.1 1.7 add_convert_fusion.5
  278.8 1.9 add_convert_fusion.3
  291.5 9.0 %all-to-all-done.2 = bf16[4,256,1152]{2,1,0:T(8,128)(2,1)S(1)} async-done(((bf16[4,256,1152]{2,1,0:T(8,128)(2,1)}), bf16[4,256,1152]{2,1,0:T(8,128)(2,1)S(1)}, u32[]{:S(2)}, u32[]{:S(2)}) %all-to-all-start.2) | async-done | bytes 2359328 | tf_op jit(solution)/shard_map/all_to_all | solution.py:831
  300.4 3.5 all-to-all-start.3
  304.0 20.2 %collective-permute-done.32 = bf16[144,2560]{1,0:T(8,128)(2,1)} collective-permute-done((bf16[144,2560]{1,0:T(8,128)(2,1)}, bf16[144,2560]{1,0:T(8,128)(2,1)}, u32[]{:S(2)}, u32[]{:S(2)}) %collective-permute-start.32) | collective-permute-done | bytes 737312 | tf_op jit(solution)/shard_map/ppermute | solution.py:57
  334.0 6.3 %finish.1 = f32[256,1152]{1,0:T(8,128)} custom-call(s32[4]{0:T(128)} %pad_add_fusion.info_ref, bf16[256,1024]{1,0:T(8,128)(2,1)} %get-tuple-element.373.refs_2_.query_ref, f32[256,512]{1,0:T(8,128)} %convert_reduce_fusion.1.refs_0_, f32[256,1152]{1,0:T(8,128)} %get-tuple-element.416.refs_1_, bf16[256,1152]{1,0:T(8,128)(2,1)} %constant_dynamic-slice_fusion.10.x_ref.refs_2_, ...), custom_call_target="tpu_custom_call" | custom-call | flops 1 | bytes 1 | tf_op jit(solution)/shard_map/finish/pallas_call | solution.py:191
  341.7 1.6 copy-done.32
  348.6 3.0 collective-permute-start.39
  353.2 2.4 collective-permute-start.37
  355.7 4.6 %add_multiply_fusion = (f32[2,144,1728]{2,1,0:T(8,128)}, f32[2,144,1728]{2,1,0:T(8,128)}, f32[2,144,1728]{2,1,0:T(8,128)}, f32[2,144,1728]{2,1,0:T(8,128)}) fusion(f32[2,144,1728]{2,1,0:T(8,128)S(1)} %copy-done.34, f32[2,144,1728]{2,1,0:T(8,128)S(1)} %copy-done.12, f32[]{:T(128)} %bitcast.66, f32[2,144,1728]{2,1,0:T(8,128)S(1)} %copy-done.35, ...), kind=kLoop, calls=%fused_computation.12 | loop fusion | flops 4478976 | bytes 15925252 | tf_op jit(solution)/shard_map/add | solution.py:51
  360.3 2.9 add_multiply_fusion.1
  (299 shorter events, 84.9 us)
Async XLA Ops:
  4.7 45.5 %collective-permute-start = (bf16[144,2816]{1,0:T(8,128)(2,1)}, bf16[144,2816]{1,0:T(8,128)(2,1)}, u32[]{:S(2)}, u32[]{:S(2)}) collective-permute-start(bf16[144,2816]{1,0:T(8,128)(2,1)} %pad_maximum_fusion.8), channel_id=1, source_target_pairs={{0,8},{4,12},{8,0},{12,4},{16,24},{20,28},{24,16},{28,20},{1,9},{5... | collective-permute-start | bytes 2433032 | tf_op jit(solution)/shard_map/ppermute | solution.py:57
  7.6 42.6 %collective-permute-start.2 = (bf16[144,2816]{1,0:T(8,128)(2,1)}, bf16[144,2816]{1,0:T(8,128)(2,1)}, u32[]{:S(2)}, u32[]{:S(2)}) collective-permute-start(bf16[144,2816]{1,0:T(8,128)(2,1)} %pad_maximum_fusion.8), channel_id=1, source_target_pairs={{0,16},{4,20},{8,24},{12,28},{16,0},{20,4},{24,8},{28,12},{1,17},{... | collective-permute-start | bytes 2433032 | tf_op jit(solution)/shard_map/ppermute | solution.py:57
  10.4 23.7 %all-to-all-start = ((bf16[4,368,256]{2,1,0:T(8,128)(2,1)}), bf16[4,368,256]{2,1,0:T(8,128)(2,1)S(1)}, u32[]{:S(2)}, u32[]{:S(2)}) async-start(bf16[4,368,256]{2,1,0:T(8,128)(2,1)} %broadcast_in_dim.11), calls=%async_computation | async-start | bytes 1507328 | tf_op jit(solution)/shard_map/all_to_all | solution.py:717
  17.0 31.7 %collective-permute-start.1 = (bf16[144,2560]{1,0:T(8,128)(2,1)}, bf16[144,2560]{1,0:T(8,128)(2,1)}, u32[]{:S(2)}, u32[]{:S(2)}) collective-permute-start(bf16[144,2560]{1,0:T(8,128)(2,1)} %pad_maximum_fusion.9), channel_id=1, source_target_pairs={{0,16},{4,20},{8,24},{12,28},{16,0},{20,4},{24,8},{28,12},{1,17},{... | collective-permute-start | bytes 2211848 | tf_op jit(solution)/shard_map/ppermute | solution.py:57
  17.5 32.7 %collective-permute-start.3 = (bf16[144,2560]{1,0:T(8,128)(2,1)}, bf16[144,2560]{1,0:T(8,128)(2,1)S(1)}, u32[]{:S(2)}, u32[]{:S(2)}) collective-permute-start(bf16[144,2560]{1,0:T(8,128)(2,1)} %pad_maximum_fusion.9), channel_id=1, source_target_pairs={{0,8},{4,12},{8,0},{12,4},{16,24},{20,28},{24,16},{28,20},{1,9},{5... | collective-permute-start | bytes 2211848 | tf_op jit(solution)/shard_map/ppermute | solution.py:57
  36.0 16.6 %all-to-all-start.1 = ((bf16[4,144,640]{2,1,0:T(8,128)(2,1)}), bf16[4,144,640]{2,1,0:T(8,128)(2,1)S(1)}, u32[]{:S(2)}, u32[]{:S(2)}) async-start(bf16[4,144,640]{2,1,0:T(8,128)(2,1)} %broadcast_in_dim.12), calls=%async_computation.1 | async-start | bytes 1474560 | tf_op jit(solution)/shard_map/all_to_all | solution.py:98
  42.5 21.4 %collective-permute-start.4 = (bf16[144,1024]{1,0:T(8,128)(2,1)}, bf16[144,1024]{1,0:T(8,128)(2,1)}, u32[]{:S(2)}, u32[]{:S(2)}) collective-permute-start(bf16[144,1024]{1,0:T(8,128)(2,1)} %pad_maximum_fusion.12), channel_id=1, source_target_pairs={{0,8},{4,12},{8,0},{12,4},{16,24},{20,28},{24,16},{28,20},{1,9},{5... | collective-permute-start | bytes 884744 | tf_op jit(solution)/shard_map/ppermute | solution.py:57
  48.7 15.3 %collective-permute-start.5 = (bf16[144,1024]{1,0:T(8,128)(2,1)}, bf16[144,1024]{1,0:T(8,128)(2,1)}, u32[]{:S(2)}, u32[]{:S(2)}) collective-permute-start(bf16[144,1024]{1,0:T(8,128)(2,1)} %pad_maximum_fusion.13), channel_id=1, source_target_pairs={{0,16},{4,20},{8,24},{12,28},{16,0},{20,4},{24,8},{28,12},{1,17},{... | collective-permute-start | bytes 884744 | tf_op jit(solution)/shard_map/ppermute | solution.py:57
  52.6 3.7 collective-permute-start.6
  54.2 32.1 %collective-permute-start.11 = (bf16[288,2816]{1,0:T(8,128)(2,1)S(1)}, bf16[288,2816]{1,0:T(8,128)(2,1)S(1)}, u32[]{:S(2)}, u32[]{:S(2)}) collective-permute-start(bf16[288,2816]{1,0:T(8,128)(2,1)S(1)} %pad_maximum_fusion.3.refs_0_), channel_id=1, source_target_pairs={{0,4},{4,0},{8,12},{12,8},{16,20},{20,16},{24,28},{28,24},{1,5},{5... | collective-permute-start | bytes 4866056 | tf_op jit(solution)/shard_map/ppermute | solution.py:57
  56.0 29.5 %collective-permute-start.12 = (bf16[288,2560]{1,0:T(8,128)(2,1)S(1)}, bf16[288,2560]{1,0:T(8,128)(2,1)S(1)}, u32[]{:S(2)}, u32[]{:S(2)}) collective-permute-start(bf16[288,2560]{1,0:T(8,128)(2,1)S(1)} %pad_maximum_fusion.4.refs_4_), channel_id=1, source_target_pairs={{0,4},{4,0},{8,12},{12,8},{16,20},{20,16},{24,28},{28,24},{1,5},{5... | collective-permute-start | bytes 4423688 | tf_op jit(solution)/shard_map/ppermute | solution.py:57
  65.2 15.5 %collective-permute-start.7 = (bf16[288,1024]{1,0:T(8,128)(2,1)S(1)}, bf16[288,1024]{1,0:T(8,128)(2,1)S(1)}, u32[]{:S(2)}, u32[]{:S(2)}) collective-permute-start(bf16[288,1024]{1,0:T(8,128)(2,1)S(1)} %pad_maximum_fusion.10), channel_id=1, source_target_pairs={{0,16},{4,20},{8,24},{12,28},{16,0},{20,4},{24,8},{28,12},{1,17},{... | collective-permute-start | bytes 1769480 | tf_op jit(solution)/shard_map/ppermute | solution.py:57
  67.9 15.2 %collective-permute-start.8 = (bf16[288,1024]{1,0:T(8,128)(2,1)S(1)}, bf16[288,1024]{1,0:T(8,128)(2,1)S(1)}, u32[]{:S(2)}, u32[]{:S(2)}) collective-permute-start(bf16[288,1024]{1,0:T(8,128)(2,1)S(1)} %pad_maximum_fusion.11), channel_id=1, source_target_pairs={{0,8},{4,12},{8,0},{12,4},{16,24},{20,28},{24,16},{28,20},{1,9},{5... | collective-permute-start | bytes 1769480 | tf_op jit(solution)/shard_map/ppermute | solution.py:57
  84.3 2.9 collective-permute-start.13
  84.4 4.5 %collective-permute-start.14 = (bf16[576,1024]{1,0:T(8,128)(2,1)S(1)}, bf16[576,1024]{1,0:T(8,128)(2,1)S(1)}, u32[]{:S(2)}, u32[]{:S(2)}) collective-permute-start(bf16[576,1024]{1,0:T(8,128)(2,1)S(1)} %pad_maximum_fusion.6.refs_2_.refs_15_), channel_id=1, source_target_pairs={{0,4},{4,0},{8,12},{12,8},{16,20},{20,16},{24,28},{28,24},{1,5},{5... | collective-permute-start | bytes 3538952 | tf_op jit(solution)/shard_map/ppermute | solution.py:57
  84.9 20.3 %collective-permute-start.9 = (bf16[144,2816]{1,0:T(8,128)(2,1)}, bf16[144,2816]{1,0:T(8,128)(2,1)S(1)}, u32[]{:S(2)}, u32[]{:S(2)}) collective-permute-start(bf16[144,2816]{1,0:T(8,128)(2,1)} %collective-permute-done), channel_id=1, source_target_pairs={{0,16},{4,20},{8,24},{12,28},{16,0},{20,4},{24,8},{28,12},{1,17},{... | collective-permute-start | bytes 2433032 | tf_op jit(solution)/shard_map/ppermute | solution.py:57
  85.6 18.4 %collective-permute-start.10 = (bf16[144,2560]{1,0:T(8,128)(2,1)}, bf16[144,2560]{1,0:T(8,128)(2,1)S(1)}, u32[]{:S(2)}, u32[]{:S(2)}) collective-permute-start(bf16[144,2560]{1,0:T(8,128)(2,1)} %collective-permute-done.1), channel_id=1, source_target_pairs={{0,8},{4,12},{8,0},{12,4},{16,24},{20,28},{24,16},{28,20},{1,9},{5... | collective-permute-start | bytes 2211848 | tf_op jit(solution)/shard_map/ppermute | solution.py:57
  106.5 5.7 %collective-permute-start.16 = (bf16[288,2816]{1,0:T(8,128)(2,1)S(1)}, bf16[288,2816]{1,0:T(8,128)(2,1)S(1)}, u32[]{:S(2)}, u32[]{:S(2)}) collective-permute-start(bf16[288,2816]{1,0:T(8,128)(2,1)S(1)} %constant_dynamic-update-slice_fusion.refs_2_), channel_id=1, source_target_pairs={{0,4},{4,0},{8,12},{12,8},{16,20},{20,16},{24,28},{28,24},{1,5},{5... | collective-permute-start | bytes 4866056 | tf_op jit(solution)/shard_map/ppermute | solution.py:57
  106.6 5.5 %collective-permute-start.17 = (bf16[288,2560]{1,0:T(8,128)(2,1)S(1)}, bf16[288,2560]{1,0:T(8,128)(2,1)S(1)}, u32[]{:S(2)}, u32[]{:S(2)}) collective-permute-start(bf16[288,2560]{1,0:T(8,128)(2,1)S(1)} %constant_dynamic-update-slice_fusion.2.refs_6_), channel_id=1, source_target_pairs={{0,4},{4,0},{8,12},{12,8},{16,20},{20,16},{24,28},{28,24},{1,5},{5... | collective-permute-start | bytes 4423688 | tf_op jit(solution)/shard_map/ppermute | solution.py:57
  107.7 26.6 %collective-permute-start.15 = (bf16[256,1152]{1,0:T(8,128)(2,1)S(1)}, bf16[256,1152]{1,0:T(8,128)(2,1)S(1)}, u32[]{:S(2)}, u32[]{:S(2)}) collective-permute-start(bf16[256,1152]{1,0:T(8,128)(2,1)S(1)} %copy-done.20), channel_id=1, source_target_pairs={{0,1},{1,0},{2,3},{3,2},{4,5},{5,4},{6,7},{7,6},{8,9},{9,8},{10,11... | collective-permute-start | bytes 1769480 | tf_op jit(solution)/shard_map/ppermute | solution.py:62
  109.2 42.4 %collective-permute-start.18 = (bf16[256,1152]{1,0:T(8,128)(2,1)S(1)}, bf16[256,1152]{1,0:T(8,128)(2,1)S(1)}, u32[]{:S(2)}, u32[]{:S(2)}) collective-permute-start(bf16[256,1152]{1,0:T(8,128)(2,1)S(1)} %copy-done.20), channel_id=1, source_target_pairs={{0,2},{1,3},{2,0},{3,1},{4,6},{5,7},{6,4},{7,5},{8,10},{9,11},{10,... | collective-permute-start | bytes 1769480 | tf_op jit(solution)/shard_map/ppermute | solution.py:62
  111.8 53.3 %collective-permute-start.19 = (bf16[256,1152]{1,0:T(8,128)(2,1)S(1)}, bf16[256,1152]{1,0:T(8,128)(2,1)}, u32[]{:S(2)}, u32[]{:S(2)}) collective-permute-start(bf16[256,1152]{1,0:T(8,128)(2,1)S(1)} %copy-done.20), channel_id=1, source_target_pairs={{0,3},{1,2},{2,1},{3,0},{4,7},{5,6},{6,5},{7,4},{8,11},{9,10},{10,... | collective-permute-start | bytes 1769480 | tf_op jit(solution)/shard_map/ppermute | solution.py:62
  151.7 29.6 %collective-permute-start.20 = (bf16[256,1152]{1,0:T(8,128)(2,1)}, bf16[256,1152]{1,0:T(8,128)(2,1)S(1)}, u32[]{:S(2)}, u32[]{:S(2)}) collective-permute-start(bf16[256,1152]{1,0:T(8,128)(2,1)} %get-tuple-element.294), channel_id=1, source_target_pairs={{0,1},{1,0},{2,3},{3,2},{4,5},{5,4},{6,7},{7,6},{8,9},{9,8},{10,11... | collective-permute-start | bytes 1769480 | tf_op jit(solution)/shard_map/ppermute | solution.py:62
  165.2 37.8 %collective-permute-start.21 = (bf16[256,1152]{1,0:T(8,128)(2,1)}, bf16[256,1152]{1,0:T(8,128)(2,1)S(1)}, u32[]{:S(2)}, u32[]{:S(2)}) collective-permute-start(bf16[256,1152]{1,0:T(8,128)(2,1)} %get-tuple-element.304), channel_id=1, source_target_pairs={{0,2},{1,3},{2,0},{3,1},{4,6},{5,7},{6,4},{7,5},{8,10},{9,11},{10,... | collective-permute-start | bytes 1769480 | tf_op jit(solution)/shard_map/ppermute | solution.py:62
  179.9 39.4 %collective-permute-start.22 = (bf16[256,1152]{1,0:T(8,128)(2,1)}, bf16[256,1152]{1,0:T(8,128)(2,1)S(1)}, u32[]{:S(2)}, u32[]{:S(2)}) collective-permute-start(bf16[256,1152]{1,0:T(8,128)(2,1)} %get-tuple-element.314), channel_id=1, source_target_pairs={{0,3},{1,2},{2,1},{3,0},{4,7},{5,6},{6,5},{7,4},{8,11},{9,10},{10,... | collective-permute-start | bytes 1769480 | tf_op jit(solution)/shard_map/ppermute | solution.py:62
  203.0 16.3 %copy-start.48 = (bf16[256,1152]{1,0:T(8,128)(2,1)}, bf16[256,1152]{1,0:T(8,128)(2,1)S(1)}, u32[]{:S(2)}) copy-start(bf16[256,1152]{1,0:T(8,128)(2,1)S(1)} %collective-permute-done.21.refs_2_) | copy-start | bytes 1769476
  220.1 10.3 %collective-permute-start.23 = (bf16[4,144,2816]{2,1,0:T(8,128)(2,1)}, bf16[4,144,2816]{2,1,0:T(8,128)(2,1)S(1)}, u32[]{:S(2)}, u32[]{:S(2)}) collective-permute-start(bf16[4,144,2816]{2,1,0:T(8,128)(2,1)} %get-tuple-element.339), channel_id=1, source_target_pairs={{0,4},{4,0},{8,12},{12,8},{16,20},{20,16},{24,28},{28,24},{1,5},{5... | collective-permute-start | bytes 9732104 | tf_op jit(solution)/shard_map/ppermute | solution.py:57
  220.1 10.3 %collective-permute-start.24 = (bf16[4,144,2560]{2,1,0:T(8,128)(2,1)}, bf16[4,144,2560]{2,1,0:T(8,128)(2,1)}, u32[]{:S(2)}, u32[]{:S(2)}) collective-permute-start(bf16[4,144,2560]{2,1,0:T(8,128)(2,1)} %get-tuple-element.340), channel_id=1, source_target_pairs={{0,4},{4,0},{8,12},{12,8},{16,20},{20,16},{24,28},{28,24},{1,5},{5... | collective-permute-start | bytes 8847368 | tf_op jit(solution)/shard_map/ppermute | solution.py:57
  238.7 37.8 %collective-permute-start.25 = (bf16[2,144,2816]{2,1,0:T(8,128)(2,1)}, bf16[2,144,2816]{2,1,0:T(8,128)(2,1)}, u32[]{:S(2)}, u32[]{:S(2)}) collective-permute-start(bf16[2,144,2816]{2,1,0:T(8,128)(2,1)} %get-tuple-element.384), channel_id=1, source_target_pairs={{0,8},{4,12},{8,0},{12,4},{16,24},{20,28},{24,16},{28,20},{1,9},{5... | collective-permute-start | bytes 4866056 | tf_op jit(solution)/shard_map/ppermute | solution.py:57
  239.3 34.4 %collective-permute-start.26 = (bf16[2,144,2560]{2,1,0:T(8,128)(2,1)}, bf16[2,144,2560]{2,1,0:T(8,128)(2,1)}, u32[]{:S(2)}, u32[]{:S(2)}) collective-permute-start(bf16[2,144,2560]{2,1,0:T(8,128)(2,1)} %get-tuple-element.385), channel_id=1, source_target_pairs={{0,16},{4,20},{8,24},{12,28},{16,0},{20,4},{24,8},{28,12},{1,17},{... | collective-permute-start | bytes 4423688 | tf_op jit(solution)/shard_map/ppermute | solution.py:57
  242.6 57.8 %all-to-all-start.2 = ((bf16[4,256,1152]{2,1,0:T(8,128)(2,1)}), bf16[4,256,1152]{2,1,0:T(8,128)(2,1)S(1)}, u32[]{:S(2)}, u32[]{:S(2)}) async-start(bf16[4,256,1152]{2,1,0:T(8,128)(2,1)} %pad_maximum_fusion.1), calls=%async_computation.2 | async-start | bytes 4718592 | tf_op jit(solution)/shard_map/all_to_all | solution.py:831
  257.7 19.3 %copy-start.16 = (bf16[2,144,2560]{2,1,0:T(8,128)(2,1)S(1)}, bf16[2,144,2560]{2,1,0:T(8,128)(2,1)}, u32[]{:S(2)}) copy-start(bf16[2,144,2560]{2,1,0:T(8,128)(2,1)} %get-tuple-element.390) | copy-start | bytes 4423684
  276.5 7.3 %collective-permute-start.27 = (bf16[4,144,1408]{2,1,0:T(8,128)(2,1)}, bf16[4,144,1408]{2,1,0:T(8,128)(2,1)S(1)}, u32[]{:S(2)}, u32[]{:S(2)}) collective-permute-start(bf16[4,144,1408]{2,1,0:T(8,128)(2,1)} %get-tuple-element.386), channel_id=1, source_target_pairs={{0,4},{4,0},{8,12},{12,8},{16,20},{20,16},{24,28},{28,24},{1,5},{5... | collective-permute-start | bytes 4866056 | tf_op jit(solution)/shard_map/ppermute | solution.py:57
  276.5 7.3 %collective-permute-start.28 = (bf16[4,144,1280]{2,1,0:T(8,128)(2,1)}, bf16[4,144,1280]{2,1,0:T(8,128)(2,1)S(1)}, u32[]{:S(2)}, u32[]{:S(2)}) collective-permute-start(bf16[4,144,1280]{2,1,0:T(8,128)(2,1)} %get-tuple-element.387), channel_id=1, source_target_pairs={{0,4},{4,0},{8,12},{12,8},{16,20},{20,16},{24,28},{28,24},{1,5},{5... | collective-permute-start | bytes 4423688 | tf_op jit(solution)/shard_map/ppermute | solution.py:57
  283.1 41.1 %collective-permute-start.31 = (bf16[144,2816]{1,0:T(8,128)(2,1)}, bf16[144,2816]{1,0:T(8,128)(2,1)}, u32[]{:S(2)}, u32[]{:S(2)}) collective-permute-start(bf16[144,2816]{1,0:T(8,128)(2,1)} %get-tuple-element.401), channel_id=1, source_target_pairs={{0,16},{4,20},{8,24},{12,28},{16,0},{20,4},{24,8},{28,12},{1,17},{... | collective-permute-start | bytes 2433032 | tf_op jit(solution)/shard_map/ppermute | solution.py:57
  288.1 36.1 %collective-permute-start.29 = (bf16[2,144,1408]{2,1,0:T(8,128)(2,1)}, bf16[2,144,1408]{2,1,0:T(8,128)(2,1)}, u32[]{:S(2)}, u32[]{:S(2)}) collective-permute-start(bf16[2,144,1408]{2,1,0:T(8,128)(2,1)} %get-tuple-element.397), channel_id=1, source_target_pairs={{0,8},{4,12},{8,0},{12,4},{16,24},{20,28},{24,16},{28,20},{1,9},{5... | collective-permute-start | bytes 2433032 | tf_op jit(solution)/shard_map/ppermute | solution.py:57
  288.8 35.3 %collective-permute-start.32 = (bf16[144,2560]{1,0:T(8,128)(2,1)}, bf16[144,2560]{1,0:T(8,128)(2,1)}, u32[]{:S(2)}, u32[]{:S(2)}) collective-permute-start(bf16[144,2560]{1,0:T(8,128)(2,1)} %get-tuple-element.402), channel_id=1, source_target_pairs={{0,8},{4,12},{8,0},{12,4},{16,24},{20,28},{24,16},{28,20},{1,9},{5... | collective-permute-start | bytes 2211848 | tf_op jit(solution)/shard_map/ppermute | solution.py:57
  290.1 34.0 %collective-permute-start.30 = (bf16[2,144,1280]{2,1,0:T(8,128)(2,1)}, bf16[2,144,1280]{2,1,0:T(8,128)(2,1)}, u32[]{:S(2)}, u32[]{:S(2)}) collective-permute-start(bf16[2,144,1280]{2,1,0:T(8,128)(2,1)} %get-tuple-element.398), channel_id=1, source_target_pairs={{0,16},{4,20},{8,24},{12,28},{16,0},{20,4},{24,8},{28,12},{1,17},{... | collective-permute-start | bytes 2211848 | tf_op jit(solution)/shard_map/ppermute | solution.py:57
  300.4 32.6 %all-to-all-start.3 = ((bf16[4,256,512]{2,1,0:T(8,128)(2,1)}), bf16[4,256,512]{2,1,0:T(8,128)(2,1)S(1)}, u32[]{:S(2)}, u32[]{:S(2)}) async-start(bf16[4,256,512]{2,1,0:T(8,128)(2,1)} %bitcast.60), calls=%async_computation.3 | async-start | bytes 2097152 | tf_op jit(solution)/shard_map/all_to_all | solution.py:868
  304.0 22.7 %copy-start.31 = (bf16[2,144,1408]{2,1,0:T(8,128)(2,1)S(1)}, bf16[2,144,1408]{2,1,0:T(8,128)(2,1)}, u32[]{:S(2)}) copy-start(bf16[2,144,1408]{2,1,0:T(8,128)(2,1)} %get-tuple-element.403) | copy-start | bytes 2433028
  329.0 11.3 %collective-permute-start.33 = (bf16[144,1408]{1,0:T(8,128)(2,1)}, bf16[144,1408]{1,0:T(8,128)(2,1)}, u32[]{:S(2)}, u32[]{:S(2)}) collective-permute-start(bf16[144,1408]{1,0:T(8,128)(2,1)} %get-tuple-element.410), channel_id=1, source_target_pairs={{0,16},{4,20},{8,24},{12,28},{16,0},{20,4},{24,8},{28,12},{1,17},{... | collective-permute-start | bytes 1216520 | tf_op jit(solution)/shard_map/ppermute | solution.py:57
  330.6 9.6 %collective-permute-start.34 = (bf16[144,1280]{1,0:T(8,128)(2,1)}, bf16[144,1280]{1,0:T(8,128)(2,1)}, u32[]{:S(2)}, u32[]{:S(2)}) collective-permute-start(bf16[144,1280]{1,0:T(8,128)(2,1)} %get-tuple-element.411), channel_id=1, source_target_pairs={{0,8},{4,12},{8,0},{12,4},{16,24},{20,28},{24,16},{28,20},{1,9},{5... | collective-permute-start | bytes 1105928 | tf_op jit(solution)/shard_map/ppermute | solution.py:57
  348.5 14.7 %collective-permute-start.38 = (bf16[36,640]{1,0:T(8,128)(2,1)S(1)}, bf16[36,640]{1,0:T(8,128)(2,1)S(1)}, u32[]{:S(2)}, u32[]{:S(2)}) collective-permute-start(bf16[36,640]{1,0:T(8,128)(2,1)S(1)} %get-tuple-element.522), channel_id=1, source_target_pairs={{0,1},{1,0},{2,3},{3,2},{4,5},{5,4},{6,7},{7,6},{8,9},{9,8},{10,11... | collective-permute-start | bytes 138248 | tf_op jit(solution)/shard_map/ppermute | solution.py:62
  348.6 15.7 %collective-permute-start.39 = (bf16[36,640]{1,0:T(8,128)(2,1)S(1)}, bf16[36,640]{1,0:T(8,128)(2,1)S(1)}, u32[]{:S(2)}, u32[]{:S(2)}) collective-permute-start(bf16[36,640]{1,0:T(8,128)(2,1)S(1)} %get-tuple-element.523), channel_id=1, source_target_pairs={{0,2},{1,3},{2,0},{3,1},{4,6},{5,7},{6,4},{7,5},{8,10},{9,11},{10,... | collective-permute-start | bytes 138248 | tf_op jit(solution)/shard_map/ppermute | solution.py:62
  351.6 12.6 %collective-permute-start.40 = (bf16[36,640]{1,0:T(8,128)(2,1)S(1)}, bf16[36,640]{1,0:T(8,128)(2,1)S(1)}, u32[]{:S(2)}, u32[]{:S(2)}) collective-permute-start(bf16[36,640]{1,0:T(8,128)(2,1)S(1)} %get-tuple-element.524), channel_id=1, source_target_pairs={{0,3},{1,2},{2,1},{3,0},{4,7},{5,6},{6,5},{7,4},{8,11},{9,10},{10,... | collective-permute-start | bytes 138248 | tf_op jit(solution)/shard_map/ppermute | solution.py:62
  353.0 16.2 %collective-permute-start.36 = (bf16[144,512]{1,0:T(8,128)(2,1)S(1)}, bf16[144,512]{1,0:T(8,128)(2,1)S(1)}, u32[]{:S(2)}, u32[]{:S(2)}) collective-permute-start(bf16[144,512]{1,0:T(8,128)(2,1)S(1)} %get-tuple-element.525), channel_id=1, source_target_pairs={{0,2},{1,3},{2,0},{3,1},{4,6},{5,7},{6,4},{7,5},{8,10},{9,11},{10,... | collective-permute-start | bytes 442376 | tf_op jit(solution)/shard_map/ppermute | solution.py:62
  353.2 16.0 %collective-permute-start.37 = (bf16[144,512]{1,0:T(8,128)(2,1)S(1)}, bf16[144,512]{1,0:T(8,128)(2,1)S(1)}, u32[]{:S(2)}, u32[]{:S(2)}) collective-permute-start(bf16[144,512]{1,0:T(8,128)(2,1)S(1)} %get-tuple-element.526), channel_id=1, source_target_pairs={{0,3},{1,2},{2,1},{3,0},{4,7},{5,6},{6,5},{7,4},{8,11},{9,10},{10,... | collective-permute-start | bytes 442376 | tf_op jit(solution)/shard_map/ppermute | solution.py:62
  363.2 6.0 %collective-permute-start.35 = (bf16[144,512]{1,0:T(8,128)(2,1)S(1)}, bf16[144,512]{1,0:T(8,128)(2,1)S(1)}, u32[]{:S(2)}, u32[]{:S(2)}) collective-permute-start(bf16[144,512]{1,0:T(8,128)(2,1)S(1)} %slice.350), channel_id=1, source_target_pairs={{0,1},{1,0},{2,3},{3,2},{4,5},{5,4},{6,7},{7,6},{8,9},{9,8},{10,11... | collective-permute-start | bytes 442376 | tf_op jit(solution)/shard_map/ppermute | solution.py:62
  (67 other events, 297.8 us)
where the time goes:
time: 378 us; the launch traced here: 372 us
  Pallas kernels  125 us (33%)
  waiting for transfers between devices  102 us (27%)
  starting transfers between devices  54.4 us (14%)
  other arithmetic  49.8 us (13%)
  local copies, waits for them, and re-layouts  38.5 us (10%)
    pallas_call x9, Pallas kernels, call(): pl.pallas_call(kernel, out_shape=out_shape, in_specs=[spaces[space] for _...  92.9 us
    ppermute x29, waiting for transfers between devices, swap(): return lax.ppermute(tensor, 'dp', [(i, i ^ bit) for i in range(count)])  62.9 us
    pallas_call x2, Pallas kernels, feed_grads(): pl.pallas_call(kernel, out_shape=(half, half), grid_spec=pltpu.PrefetchSc...  31.6 us
    ppermute x29, starting transfers between devices, swap(): return lax.ppermute(tensor, 'dp', [(i, i ^ bit) for i in range(count)])  22 us
    unnamed x142, local copies, waits for them, and re-layouts  19.3 us
    ppermute x12, waiting for transfers between devices, across_heads(): return lax.ppermute(tensor, 'mp', [(i, i ^ bit) for i in range(count)])  17.1 us
    ppermute x12, starting transfers between devices, across_heads(): return lax.ppermute(tensor, 'mp', [(i, i ^ bit) for i in range(count)])  16.2 us
    add x6, other arithmetic, advance(): average_new = AVERAGING * average + (1.0 - AVERAGING) * weight_new  12.3 us
  transfers between devices with their start and end apart: 45, of which 18 were waited for; matrix products, arithmetic and copies ran while one was open for 14% of the time, Pallas kernels for 33%

commit v1 on v0

--- a/solution.py
+++ b/solution.py
@@ -124,7 +124,7 @@
 
 def column_cuts(width):
     half = round_up(width // TILE, 2) // 2 * TILE
-    first = round_up(half // TILE, 2) // 2 * TILE
+    first = TILE
     return half, [(0, first), (first, half), (half, width)]
 
 

time: 378 us -> 380 us (level)
  Pallas kernels: 125 us -> 131 us
  waiting for transfers between devices: 102 us -> 97.7 us
    pallas_call x9, Pallas kernels: 92.9 us -> 99.9 us  [call(): pl.pallas_call(kernel, out_shape=out_shape, in_specs=[spaces[space] for _...]
    ppermute x12, waiting for transfers between devices: 17.1 us -> 13 us  [across_heads(): return lax.ppermute(tensor, 'mp', [(i, i ^ bit) for i in range(count)])]
  transfers between devices with their start and end apart: 45 -> 45, of which waited for: 18 -> 18; matrix products, arithmetic and copies ran while one was open for 14% -> 14% of each run, Pallas kernels for 33% -> 35%
where the time goes in v1:
time: 380 us; the launch traced here: 375 us
  Pallas kernels  131 us (34%)
  waiting for transfers between devices  97.7 us (26%)
  starting transfers between devices  55.2 us (15%)
  other arithmetic  49.8 us (13%)
  local copies, waits for them, and re-layouts  38.5 us (10%)
    pallas_call x9, Pallas kernels, call(): pl.pallas_call(kernel, out_shape=out_shape, in_specs=[spaces[space] for _...  99.9 us
    ppermute x29, waiting for transfers between devices, swap(): return lax.ppermute(tensor, 'dp', [(i, i ^ bit) for i in range(count)])  61.8 us
    pallas_call x2, Pallas kernels, feed_grads(): pl.pallas_call(kernel, out_shape=(half, half), grid_spec=pltpu.PrefetchSc...  31.4 us
    ppermute x29, starting transfers between devices, swap(): return lax.ppermute(tensor, 'dp', [(i, i ^ bit) for i in range(count)])  22 us
    unnamed x142, local copies, waits for them, and re-layouts  19.3 us
    ppermute x12, starting transfers between devices, across_heads(): return lax.ppermute(tensor, 'mp', [(i, i ^ bit) for i in range(count)])  16.4 us
    ppermute x12, waiting for transfers between devices, across_heads(): return lax.ppermute(tensor, 'mp', [(i, i ^ bit) for i in range(count)])  13 us
    add x6, other arithmetic, advance(): average_new = AVERAGING * average + (1.0 - AVERAGING) * weight_new  12.3 us
  transfers between devices with their start and end apart: 45, of which 18 were waited for; matrix products, arithmetic and copies ran while one was open for 14% of the time, Pallas kernels for 35%

profile of v1, /device:TPU:0, one launch (start us, length us, event | category | flops | bytes accessed | tf_op | source)
XLA Modules:
  0.0 375.2 jit_solution(12901557539178585183)
XLA Ops:
  0.7 1.7 convert_element_type.219
  4.7 2.9 collective-permute-start
  10.4 4.9 %all-to-all-start = ((bf16[4,368,256]{2,1,0:T(8,128)(2,1)}), bf16[4,368,256]{2,1,0:T(8,128)(2,1)S(1)}, u32[]{:S(2)}, u32[]{:S(2)}) async-start(bf16[4,368,256]{2,1,0:T(8,128)(2,1)} %broadcast_in_dim.11), calls=%async_computation | async-start | bytes 1507328 | tf_op jit(solution)/shard_map/all_to_all | solution.py:717
  19.4 1.9 multiply_sine_fusion
  22.9 11.1 %all-to-all-done = bf16[4,368,256]{2,1,0:T(8,128)(2,1)S(1)} async-done(((bf16[4,368,256]{2,1,0:T(8,128)(2,1)}), bf16[4,368,256]{2,1,0:T(8,128)(2,1)S(1)}, u32[]{:S(2)}, u32[]{:S(2)}) %all-to-all-start) | async-done | bytes 753696 | tf_op jit(solution)/shard_map/all_to_all | solution.py:717
  36.0 3.8 %all-to-all-start.1 = ((bf16[4,144,640]{2,1,0:T(8,128)(2,1)}), bf16[4,144,640]{2,1,0:T(8,128)(2,1)S(1)}, u32[]{:S(2)}, u32[]{:S(2)}) async-start(bf16[4,144,640]{2,1,0:T(8,128)(2,1)} %broadcast_in_dim.12), calls=%async_computation.1 | async-start | bytes 1474560 | tf_op jit(solution)/shard_map/all_to_all | solution.py:98
  39.8 2.0 constant_dynamic-slice_fusion.10.x_ref.refs_2_
  42.5 2.0 collective-permute-start.4
  45.2 3.5 collective-permute-done.1
  50.2 2.3 all-to-all-done.1
  57.3 6.6 %project.1 = (bf16[1024,1152]{1,0:T(8,128)(2,1)}, bf16[256,1152]{1,0:T(8,128)(2,1)}, bf16[1024,256]{1,0:T(8,128)(2,1)}, bf16[1024,256]{1,0:T(8,128)(2,1)}, f32[8,1152]{1,0:T(8,128)}) custom-call(s32[4]{0:T(128)} %pad_add_fusion.info_ref, bf16[1024,1152]{1,0:T(8,128)(2,1)} %x_ref.1, f32[1024,128]{1,0:T(8,128)} %copy-done.19, f32[1024,128]{1,0:T(8,128)} %copy-done.18, ...), custom_call_target="tpu_custom_call" | custom-call | flops 1 | bytes 1 | tf_op jit(solution)/shard_map/project/pallas_call | solution.py:191
  65.2 1.6 collective-permute-start.7
  69.8 10.9 %collective-permute-done.7 = bf16[288,1024]{1,0:T(8,128)(2,1)S(1)} collective-permute-done((bf16[288,1024]{1,0:T(8,128)(2,1)S(1)}, bf16[288,1024]{1,0:T(8,128)(2,1)S(1)}, u32[]{:S(2)}, u32[]{:S(2)}) %collective-permute-start.7) | collective-permute-done | bytes 589856 | tf_op jit(solution)/shard_map/ppermute | solution.py:57
  89.9 8.6 %attend.1 = (bf16[256,1024]{1,0:T(8,128)(2,1)}, bf16[256,1024]{1,0:T(8,128)(2,1)}, f32[256,1152]{1,0:T(8,128)}, bf16[256,1152]{1,0:T(8,128)(2,1)}, f32[256,128]{1,0:T(8,128)}) custom-call(s32[4]{0:T(128)} %pad_add_fusion.info_ref, bf16[256,1152]{1,0:T(8,128)(2,1)} %get-tuple-element.372.own_ref.refs_1_, ...), custom_call_target="tpu_custom_call" | custom-call | flops 1 | bytes 1 | tf_op jit(solution)/shard_map/attend/pallas_call | solution.py:191
  98.6 5.4 %collective-permute-done.10 = bf16[144,2560]{1,0:T(8,128)(2,1)S(1)} collective-permute-done((bf16[144,2560]{1,0:T(8,128)(2,1)}, bf16[144,2560]{1,0:T(8,128)(2,1)S(1)}, u32[]{:S(2)}, u32[]{:S(2)}) %collective-permute-start.10) | collective-permute-done | bytes 737312 | tf_op jit(solution)/shard_map/ppermute | solution.py:57
  107.7 1.6 collective-permute-start.15
  109.2 2.6 collective-permute-start.18
  114.4 14.8 %feed_block.4 = (bf16[256,1792]{1,0:T(8,128)(2,1)}, bf16[256,1792]{1,0:T(8,128)(2,1)}, bf16[256,1792]{1,0:T(8,128)(2,1)}, f32[256,1152]{1,0:T(8,128)}, f32[256,1152]{1,0:T(8,128)}) custom-call(s32[4]{0:T(128)} %pad_add_fusion.info_ref, bf16[256,1152]{1,0:T(8,128)(2,1)} %get-tuple-element.255.x_ref.refs_0_, ...), custom_call_target="tpu_custom_call" | custom-call | flops 1 | bytes 1 | tf_op jit(solution)/shard_map/feed_block/pallas_call | solution.py:191
  129.3 5.0 %collective-permute-done.15.x_ref.refs_1_ = bf16[256,1152]{1,0:T(8,128)(2,1)S(1)} collective-permute-done((bf16[256,1152]{1,0:T(8,128)(2,1)S(1)}, bf16[256,1152]{1,0:T(8,128)(2,1)S(1)}, u32[]{:S(2)}, u32[]{:S(2)}) %collective-permute-start.15) | collective-permute-done | bytes 589856 | tf_op jit(solution)/shard_map/ppermute | solution.py:62
  135.1 14.2 %feed_block.5 = (bf16[256,1792]{1,0:T(8,128)(2,1)}, bf16[256,1792]{1,0:T(8,128)(2,1)}, bf16[256,1792]{1,0:T(8,128)(2,1)}, bf16[256,1152]{1,0:T(8,128)(2,1)}, bf16[256,1152]{1,0:T(8,128)(2,1)}) custom-call(s32[4]{0:T(128)} %pad_add_fusion.info_ref, bf16[256,1152]{1,0:T(8,128)(2,1)} %copy-done.21, bf16[256,1152]{1,0:T(8,128)(2,1)} %get-tuple-element.271.g_ref.refs_9_, ...), custom_call_target="tpu_custom_call" | custom-call | flops 1 | bytes 1 | tf_op jit(solution)/shard_map/feed_block/pallas_call | solution.py:191
  149.3 2.4 collective-permute-done.18.x_ref.refs_2_
  152.5 14.3 %feed_block.6 = (bf16[256,1792]{1,0:T(8,128)(2,1)}, bf16[256,1792]{1,0:T(8,128)(2,1)}, bf16[256,1792]{1,0:T(8,128)(2,1)}, bf16[256,1152]{1,0:T(8,128)(2,1)}, bf16[256,1152]{1,0:T(8,128)(2,1)}) custom-call(s32[4]{0:T(128)} %pad_add_fusion.info_ref, bf16[256,1152]{1,0:T(8,128)(2,1)} %copy-done.22, bf16[256,1152]{1,0:T(8,128)(2,1)} %get-tuple-element.278.g_ref.refs_10_, ...), custom_call_target="tpu_custom_call" | custom-call | flops 1 | bytes 1 | tf_op jit(solution)/shard_map/feed_block/pallas_call | solution.py:191
  166.9 2.3 collective-permute-start.21
  169.2 14.3 %feed_block.7 = (bf16[256,1792]{1,0:T(8,128)(2,1)}, bf16[256,1792]{1,0:T(8,128)(2,1)}, bf16[256,1792]{1,0:T(8,128)(2,1)}, bf16[256,1152]{1,0:T(8,128)(2,1)}, bf16[256,1152]{1,0:T(8,128)(2,1)}) custom-call(s32[4]{0:T(128)} %pad_add_fusion.info_ref, bf16[256,1152]{1,0:T(8,128)(2,1)} %collective-permute-done.19.x_ref.refs_3_, ...), custom_call_target="tpu_custom_call" | custom-call | flops 1 | bytes 1 | tf_op jit(solution)/shard_map/feed_block/pallas_call | solution.py:191
  184.9 15.1 %feed_grads.2 = (bf16[4,144,2560]{2,1,0:T(8,128)(2,1)}, bf16[4,144,2560]{2,1,0:T(8,128)(2,1)}) custom-call(s32[4]{0:T(128)} %pad_add_fusion.info_ref, bf16[256,1152]{1,0:T(8,128)(2,1)} %get-tuple-element.255.x_ref.refs_0_, bf16[256,1152]{1,0:T(8,128)(2,1)} %copy-done.21, bf16[256,1152]{1,0:T(8,128)(2,1)} %copy-done.22, ...), custom_call_target="tpu_custom_call" | custom-call | flops 1 | bytes 1 | tf_op jit(solution)/shard_map/feed_grads/pallas_call | solution.py:597
  200.0 5.6 %collective-permute-done.21.refs_2_ = bf16[256,1152]{1,0:T(8,128)(2,1)S(1)} collective-permute-done((bf16[256,1152]{1,0:T(8,128)(2,1)}, bf16[256,1152]{1,0:T(8,128)(2,1)S(1)}, u32[]{:S(2)}, u32[]{:S(2)}) %collective-permute-start.21) | collective-permute-done | bytes 589856 | tf_op jit(solution)/shard_map/ppermute | solution.py:62
  205.6 16.3 %feed_grads.3 = (bf16[4,144,2816]{2,1,0:T(8,128)(2,1)}, bf16[4,144,2816]{2,1,0:T(8,128)(2,1)}) custom-call(s32[4]{0:T(128)} %pad_add_fusion.info_ref, bf16[256,1152]{1,0:T(8,128)(2,1)} %get-tuple-element.255.x_ref.refs_0_, bf16[256,1152]{1,0:T(8,128)(2,1)} %copy-done.21, bf16[256,1152]{1,0:T(8,128)(2,1)} %copy-done.22, ...), custom_call_target="tpu_custom_call" | custom-call | flops 1 | bytes 1 | tf_op jit(solution)/shard_map/feed_grads/pallas_call | solution.py:597
  223.3 9.8 %collective-permute-done.24 = bf16[4,144,2560]{2,1,0:T(8,128)(2,1)} collective-permute-done((bf16[4,144,2560]{2,1,0:T(8,128)(2,1)}, bf16[4,144,2560]{2,1,0:T(8,128)(2,1)}, u32[]{:S(2)}, u32[]{:S(2)}) %collective-permute-start.24) | collective-permute-done | bytes 2949152 | tf_op jit(solution)/shard_map/ppermute | solution.py:57
  233.1 3.6 add_convert_fusion.1
  237.6 1.8 dynamic-slice_bitcast_fusion.2
  239.5 1.9 dynamic-slice_bitcast_fusion
  243.5 1.7 pad_maximum_fusion.1
  245.2 4.7 %all-to-all-start.2 = ((bf16[4,256,1152]{2,1,0:T(8,128)(2,1)}), bf16[4,256,1152]{2,1,0:T(8,128)(2,1)S(1)}, u32[]{:S(2)}, u32[]{:S(2)}) async-start(bf16[4,256,1152]{2,1,0:T(8,128)(2,1)} %pad_maximum_fusion.1), calls=%async_computation.2 | async-start | bytes 4718592 | tf_op jit(solution)/shard_map/all_to_all | solution.py:831
  250.0 11.0 %attend_back.1 = (f32[256,1152]{1,0:T(8,128)}, bf16[256,1152]{1,0:T(8,128)(2,1)}, f32[8,1152]{1,0:T(8,128)}, bf16[256,1024]{1,0:T(8,128)(2,1)}, bf16[1024,512]{1,0:T(8,128)(2,1)}) custom-call(s32[4]{0:T(128)} %pad_add_fusion.info_ref, f32[256,1152]{1,0:T(8,128)} %get-tuple-element.349.refs_0_, bf16[256,1152]{1,0:T(8,128)(2,1)} %copy-done.47, ...), custom_call_target="tpu_custom_call" | custom-call | flops 1 | bytes 1 | tf_op jit(solution)/shard_map/attend_back/pallas_call | solution.py:191
  261.0 9.7 %mixer_grads.1 = (bf16[4,144,1408]{2,1,0:T(8,128)(2,1)}, bf16[4,144,1408]{2,1,0:T(8,128)(2,1)}, bf16[4,144,1280]{2,1,0:T(8,128)(2,1)}, bf16[4,144,1280]{2,1,0:T(8,128)(2,1)}) custom-call(s32[4]{0:T(128)} %pad_add_fusion.info_ref, bf16[1024,1152]{1,0:T(8,128)(2,1)} %get-tuple-element.371.refs_0_, bf16[256,1152]{1,0:T(8,128)(2,1)} %get-tuple-element.372.own_ref.refs_1_, ...), custom_call_target="tpu_custom_call" | custom-call | flops 1 | bytes 1 | tf_op jit(solution)/shard_map/mixer_grads/pallas_call | solution.py:191
  270.7 5.6 %collective-permute-done.26 = bf16[2,144,2560]{2,1,0:T(8,128)(2,1)} collective-permute-done((bf16[2,144,2560]{2,1,0:T(8,128)(2,1)}, bf16[2,144,2560]{2,1,0:T(8,128)(2,1)}, u32[]{:S(2)}, u32[]{:S(2)}) %collective-permute-start.26) | collective-permute-done | bytes 1474592 | tf_op jit(solution)/shard_map/ppermute | solution.py:57
  276.3 2.9 collective-permute-done.25
  279.7 1.7 add_convert_fusion.5
  281.4 1.9 add_convert_fusion.3
  294.1 9.4 %all-to-all-done.2 = bf16[4,256,1152]{2,1,0:T(8,128)(2,1)S(1)} async-done(((bf16[4,256,1152]{2,1,0:T(8,128)(2,1)}), bf16[4,256,1152]{2,1,0:T(8,128)(2,1)S(1)}, u32[]{:S(2)}, u32[]{:S(2)}) %all-to-all-start.2) | async-done | bytes 2359328 | tf_op jit(solution)/shard_map/all_to_all | solution.py:831
  303.6 3.5 all-to-all-start.3
  307.1 19.7 %collective-permute-done.32 = bf16[144,2560]{1,0:T(8,128)(2,1)} collective-permute-done((bf16[144,2560]{1,0:T(8,128)(2,1)}, bf16[144,2560]{1,0:T(8,128)(2,1)}, u32[]{:S(2)}, u32[]{:S(2)}) %collective-permute-start.32) | collective-permute-done | bytes 737312 | tf_op jit(solution)/shard_map/ppermute | solution.py:57
  336.6 6.3 %finish.1 = f32[256,1152]{1,0:T(8,128)} custom-call(s32[4]{0:T(128)} %pad_add_fusion.info_ref, bf16[256,1024]{1,0:T(8,128)(2,1)} %get-tuple-element.373.refs_2_.query_ref, f32[256,512]{1,0:T(8,128)} %convert_reduce_fusion.1.refs_0_, f32[256,1152]{1,0:T(8,128)} %get-tuple-element.416.refs_1_, bf16[256,1152]{1,0:T(8,128)(2,1)} %constant_dynamic-slice_fusion.10.x_ref.refs_2_, ...), custom_call_target="tpu_custom_call" | custom-call | flops 1 | bytes 1 | tf_op jit(solution)/shard_map/finish/pallas_call | solution.py:191
  344.4 1.6 copy-done.32
  351.6 3.3 collective-permute-start.39
  356.5 2.4 collective-permute-start.37
  358.9 4.6 %add_multiply_fusion = (f32[2,144,1728]{2,1,0:T(8,128)}, f32[2,144,1728]{2,1,0:T(8,128)}, f32[2,144,1728]{2,1,0:T(8,128)}, f32[2,144,1728]{2,1,0:T(8,128)}) fusion(f32[2,144,1728]{2,1,0:T(8,128)S(1)} %copy-done.34, f32[2,144,1728]{2,1,0:T(8,128)S(1)} %copy-done.12, f32[]{:T(128)} %bitcast.66, f32[2,144,1728]{2,1,0:T(8,128)S(1)} %copy-done.35, ...), kind=kLoop, calls=%fused_computation.12 | loop fusion | flops 4478976 | bytes 15925252 | tf_op jit(solution)/shard_map/add | solution.py:51
  363.5 2.9 add_multiply_fusion.1
  (299 shorter events, 84.8 us)
Async XLA Ops:
  4.7 45.5 %collective-permute-start = (bf16[144,2816]{1,0:T(8,128)(2,1)}, bf16[144,2816]{1,0:T(8,128)(2,1)}, u32[]{:S(2)}, u32[]{:S(2)}) collective-permute-start(bf16[144,2816]{1,0:T(8,128)(2,1)} %pad_maximum_fusion.8), channel_id=1, source_target_pairs={{0,8},{4,12},{8,0},{12,4},{16,24},{20,28},{24,16},{28,20},{1,9},{5... | collective-permute-start | bytes 2433032 | tf_op jit(solution)/shard_map/ppermute | solution.py:57
  7.6 42.6 %collective-permute-start.2 = (bf16[144,2816]{1,0:T(8,128)(2,1)}, bf16[144,2816]{1,0:T(8,128)(2,1)}, u32[]{:S(2)}, u32[]{:S(2)}) collective-permute-start(bf16[144,2816]{1,0:T(8,128)(2,1)} %pad_maximum_fusion.8), channel_id=1, source_target_pairs={{0,16},{4,20},{8,24},{12,28},{16,0},{20,4},{24,8},{28,12},{1,17},{... | collective-permute-start | bytes 2433032 | tf_op jit(solution)/shard_map/ppermute | solution.py:57
  10.4 23.7 %all-to-all-start = ((bf16[4,368,256]{2,1,0:T(8,128)(2,1)}), bf16[4,368,256]{2,1,0:T(8,128)(2,1)S(1)}, u32[]{:S(2)}, u32[]{:S(2)}) async-start(bf16[4,368,256]{2,1,0:T(8,128)(2,1)} %broadcast_in_dim.11), calls=%async_computation | async-start | bytes 1507328 | tf_op jit(solution)/shard_map/all_to_all | solution.py:717
  17.0 31.7 %collective-permute-start.1 = (bf16[144,2560]{1,0:T(8,128)(2,1)}, bf16[144,2560]{1,0:T(8,128)(2,1)}, u32[]{:S(2)}, u32[]{:S(2)}) collective-permute-start(bf16[144,2560]{1,0:T(8,128)(2,1)} %pad_maximum_fusion.9), channel_id=1, source_target_pairs={{0,16},{4,20},{8,24},{12,28},{16,0},{20,4},{24,8},{28,12},{1,17},{... | collective-permute-start | bytes 2211848 | tf_op jit(solution)/shard_map/ppermute | solution.py:57
  17.5 32.7 %collective-permute-start.3 = (bf16[144,2560]{1,0:T(8,128)(2,1)}, bf16[144,2560]{1,0:T(8,128)(2,1)S(1)}, u32[]{:S(2)}, u32[]{:S(2)}) collective-permute-start(bf16[144,2560]{1,0:T(8,128)(2,1)} %pad_maximum_fusion.9), channel_id=1, source_target_pairs={{0,8},{4,12},{8,0},{12,4},{16,24},{20,28},{24,16},{28,20},{1,9},{5... | collective-permute-start | bytes 2211848 | tf_op jit(solution)/shard_map/ppermute | solution.py:57
  36.0 16.6 %all-to-all-start.1 = ((bf16[4,144,640]{2,1,0:T(8,128)(2,1)}), bf16[4,144,640]{2,1,0:T(8,128)(2,1)S(1)}, u32[]{:S(2)}, u32[]{:S(2)}) async-start(bf16[4,144,640]{2,1,0:T(8,128)(2,1)} %broadcast_in_dim.12), calls=%async_computation.1 | async-start | bytes 1474560 | tf_op jit(solution)/shard_map/all_to_all | solution.py:98
  42.5 21.4 %collective-permute-start.4 = (bf16[144,1024]{1,0:T(8,128)(2,1)}, bf16[144,1024]{1,0:T(8,128)(2,1)}, u32[]{:S(2)}, u32[]{:S(2)}) collective-permute-start(bf16[144,1024]{1,0:T(8,128)(2,1)} %pad_maximum_fusion.12), channel_id=1, source_target_pairs={{0,8},{4,12},{8,0},{12,4},{16,24},{20,28},{24,16},{28,20},{1,9},{5... | collective-permute-start | bytes 884744 | tf_op jit(solution)/shard_map/ppermute | solution.py:57
  48.7 15.3 %collective-permute-start.5 = (bf16[144,1024]{1,0:T(8,128)(2,1)}, bf16[144,1024]{1,0:T(8,128)(2,1)}, u32[]{:S(2)}, u32[]{:S(2)}) collective-permute-start(bf16[144,1024]{1,0:T(8,128)(2,1)} %pad_maximum_fusion.13), channel_id=1, source_target_pairs={{0,16},{4,20},{8,24},{12,28},{16,0},{20,4},{24,8},{28,12},{1,17},{... | collective-permute-start | bytes 884744 | tf_op jit(solution)/shard_map/ppermute | solution.py:57
  52.6 3.7 collective-permute-start.6
  54.2 32.1 %collective-permute-start.11 = (bf16[288,2816]{1,0:T(8,128)(2,1)S(1)}, bf16[288,2816]{1,0:T(8,128)(2,1)S(1)}, u32[]{:S(2)}, u32[]{:S(2)}) collective-permute-start(bf16[288,2816]{1,0:T(8,128)(2,1)S(1)} %pad_maximum_fusion.3.refs_0_), channel_id=1, source_target_pairs={{0,4},{4,0},{8,12},{12,8},{16,20},{20,16},{24,28},{28,24},{1,5},{5... | collective-permute-start | bytes 4866056 | tf_op jit(solution)/shard_map/ppermute | solution.py:57
  56.0 29.5 %collective-permute-start.12 = (bf16[288,2560]{1,0:T(8,128)(2,1)S(1)}, bf16[288,2560]{1,0:T(8,128)(2,1)S(1)}, u32[]{:S(2)}, u32[]{:S(2)}) collective-permute-start(bf16[288,2560]{1,0:T(8,128)(2,1)S(1)} %pad_maximum_fusion.4.refs_4_), channel_id=1, source_target_pairs={{0,4},{4,0},{8,12},{12,8},{16,20},{20,16},{24,28},{28,24},{1,5},{5... | collective-permute-start | bytes 4423688 | tf_op jit(solution)/shard_map/ppermute | solution.py:57
  65.2 15.5 %collective-permute-start.7 = (bf16[288,1024]{1,0:T(8,128)(2,1)S(1)}, bf16[288,1024]{1,0:T(8,128)(2,1)S(1)}, u32[]{:S(2)}, u32[]{:S(2)}) collective-permute-start(bf16[288,1024]{1,0:T(8,128)(2,1)S(1)} %pad_maximum_fusion.10), channel_id=1, source_target_pairs={{0,16},{4,20},{8,24},{12,28},{16,0},{20,4},{24,8},{28,12},{1,17},{... | collective-permute-start | bytes 1769480 | tf_op jit(solution)/shard_map/ppermute | solution.py:57
  67.9 15.2 %collective-permute-start.8 = (bf16[288,1024]{1,0:T(8,128)(2,1)S(1)}, bf16[288,1024]{1,0:T(8,128)(2,1)S(1)}, u32[]{:S(2)}, u32[]{:S(2)}) collective-permute-start(bf16[288,1024]{1,0:T(8,128)(2,1)S(1)} %pad_maximum_fusion.11), channel_id=1, source_target_pairs={{0,8},{4,12},{8,0},{12,4},{16,24},{20,28},{24,16},{28,20},{1,9},{5... | collective-permute-start | bytes 1769480 | tf_op jit(solution)/shard_map/ppermute | solution.py:57
  84.3 2.9 collective-permute-start.13
  84.4 4.5 %collective-permute-start.14 = (bf16[576,1024]{1,0:T(8,128)(2,1)S(1)}, bf16[576,1024]{1,0:T(8,128)(2,1)S(1)}, u32[]{:S(2)}, u32[]{:S(2)}) collective-permute-start(bf16[576,1024]{1,0:T(8,128)(2,1)S(1)} %pad_maximum_fusion.6.refs_2_.refs_15_), channel_id=1, source_target_pairs={{0,4},{4,0},{8,12},{12,8},{16,20},{20,16},{24,28},{28,24},{1,5},{5... | collective-permute-start | bytes 3538952 | tf_op jit(solution)/shard_map/ppermute | solution.py:57
  84.9 20.3 %collective-permute-start.9 = (bf16[144,2816]{1,0:T(8,128)(2,1)}, bf16[144,2816]{1,0:T(8,128)(2,1)S(1)}, u32[]{:S(2)}, u32[]{:S(2)}) collective-permute-start(bf16[144,2816]{1,0:T(8,128)(2,1)} %collective-permute-done), channel_id=1, source_target_pairs={{0,16},{4,20},{8,24},{12,28},{16,0},{20,4},{24,8},{28,12},{1,17},{... | collective-permute-start | bytes 2433032 | tf_op jit(solution)/shard_map/ppermute | solution.py:57
  85.6 18.4 %collective-permute-start.10 = (bf16[144,2560]{1,0:T(8,128)(2,1)}, bf16[144,2560]{1,0:T(8,128)(2,1)S(1)}, u32[]{:S(2)}, u32[]{:S(2)}) collective-permute-start(bf16[144,2560]{1,0:T(8,128)(2,1)} %collective-permute-done.1), channel_id=1, source_target_pairs={{0,8},{4,12},{8,0},{12,4},{16,24},{20,28},{24,16},{28,20},{1,9},{5... | collective-permute-start | bytes 2211848 | tf_op jit(solution)/shard_map/ppermute | solution.py:57
  106.5 5.7 %collective-permute-start.16 = (bf16[288,2816]{1,0:T(8,128)(2,1)S(1)}, bf16[288,2816]{1,0:T(8,128)(2,1)S(1)}, u32[]{:S(2)}, u32[]{:S(2)}) collective-permute-start(bf16[288,2816]{1,0:T(8,128)(2,1)S(1)} %constant_dynamic-update-slice_fusion.refs_2_), channel_id=1, source_target_pairs={{0,4},{4,0},{8,12},{12,8},{16,20},{20,16},{24,28},{28,24},{1,5},{5... | collective-permute-start | bytes 4866056 | tf_op jit(solution)/shard_map/ppermute | solution.py:57
  106.6 5.5 %collective-permute-start.17 = (bf16[288,2560]{1,0:T(8,128)(2,1)S(1)}, bf16[288,2560]{1,0:T(8,128)(2,1)S(1)}, u32[]{:S(2)}, u32[]{:S(2)}) collective-permute-start(bf16[288,2560]{1,0:T(8,128)(2,1)S(1)} %constant_dynamic-update-slice_fusion.2.refs_6_), channel_id=1, source_target_pairs={{0,4},{4,0},{8,12},{12,8},{16,20},{20,16},{24,28},{28,24},{1,5},{5... | collective-permute-start | bytes 4423688 | tf_op jit(solution)/shard_map/ppermute | solution.py:57
  107.7 26.6 %collective-permute-start.15 = (bf16[256,1152]{1,0:T(8,128)(2,1)S(1)}, bf16[256,1152]{1,0:T(8,128)(2,1)S(1)}, u32[]{:S(2)}, u32[]{:S(2)}) collective-permute-start(bf16[256,1152]{1,0:T(8,128)(2,1)S(1)} %copy-done.20), channel_id=1, source_target_pairs={{0,1},{1,0},{2,3},{3,2},{4,5},{5,4},{6,7},{7,6},{8,9},{9,8},{10,11... | collective-permute-start | bytes 1769480 | tf_op jit(solution)/shard_map/ppermute | solution.py:62
  109.2 42.4 %collective-permute-start.18 = (bf16[256,1152]{1,0:T(8,128)(2,1)S(1)}, bf16[256,1152]{1,0:T(8,128)(2,1)S(1)}, u32[]{:S(2)}, u32[]{:S(2)}) collective-permute-start(bf16[256,1152]{1,0:T(8,128)(2,1)S(1)} %copy-done.20), channel_id=1, source_target_pairs={{0,2},{1,3},{2,0},{3,1},{4,6},{5,7},{6,4},{7,5},{8,10},{9,11},{10,... | collective-permute-start | bytes 1769480 | tf_op jit(solution)/shard_map/ppermute | solution.py:62
  111.8 55.0 %collective-permute-start.19 = (bf16[256,1152]{1,0:T(8,128)(2,1)S(1)}, bf16[256,1152]{1,0:T(8,128)(2,1)}, u32[]{:S(2)}, u32[]{:S(2)}) collective-permute-start(bf16[256,1152]{1,0:T(8,128)(2,1)S(1)} %copy-done.20), channel_id=1, source_target_pairs={{0,3},{1,2},{2,1},{3,0},{4,7},{5,6},{6,5},{7,4},{8,11},{9,10},{10,... | collective-permute-start | bytes 1769480 | tf_op jit(solution)/shard_map/ppermute | solution.py:62
  151.7 33.2 %collective-permute-start.20 = (bf16[256,1152]{1,0:T(8,128)(2,1)}, bf16[256,1152]{1,0:T(8,128)(2,1)S(1)}, u32[]{:S(2)}, u32[]{:S(2)}) collective-permute-start(bf16[256,1152]{1,0:T(8,128)(2,1)} %get-tuple-element.294), channel_id=1, source_target_pairs={{0,1},{1,0},{2,3},{3,2},{4,5},{5,4},{6,7},{7,6},{8,9},{9,8},{10,11... | collective-permute-start | bytes 1769480 | tf_op jit(solution)/shard_map/ppermute | solution.py:62
  166.9 38.8 %collective-permute-start.21 = (bf16[256,1152]{1,0:T(8,128)(2,1)}, bf16[256,1152]{1,0:T(8,128)(2,1)S(1)}, u32[]{:S(2)}, u32[]{:S(2)}) collective-permute-start(bf16[256,1152]{1,0:T(8,128)(2,1)} %get-tuple-element.304), channel_id=1, source_target_pairs={{0,2},{1,3},{2,0},{3,1},{4,6},{5,7},{6,4},{7,5},{8,10},{9,11},{10,... | collective-permute-start | bytes 1769480 | tf_op jit(solution)/shard_map/ppermute | solution.py:62
  183.5 38.4 %collective-permute-start.22 = (bf16[256,1152]{1,0:T(8,128)(2,1)}, bf16[256,1152]{1,0:T(8,128)(2,1)S(1)}, u32[]{:S(2)}, u32[]{:S(2)}) collective-permute-start(bf16[256,1152]{1,0:T(8,128)(2,1)} %get-tuple-element.314), channel_id=1, source_target_pairs={{0,3},{1,2},{2,1},{3,0},{4,7},{5,6},{6,5},{7,4},{8,11},{9,10},{10,... | collective-permute-start | bytes 1769480 | tf_op jit(solution)/shard_map/ppermute | solution.py:62
  205.6 16.3 %copy-start.48 = (bf16[256,1152]{1,0:T(8,128)(2,1)}, bf16[256,1152]{1,0:T(8,128)(2,1)S(1)}, u32[]{:S(2)}) copy-start(bf16[256,1152]{1,0:T(8,128)(2,1)S(1)} %collective-permute-done.21.refs_2_) | copy-start | bytes 1769476
  222.8 10.3 %collective-permute-start.23 = (bf16[4,144,2816]{2,1,0:T(8,128)(2,1)}, bf16[4,144,2816]{2,1,0:T(8,128)(2,1)S(1)}, u32[]{:S(2)}, u32[]{:S(2)}) collective-permute-start(bf16[4,144,2816]{2,1,0:T(8,128)(2,1)} %get-tuple-element.339), channel_id=1, source_target_pairs={{0,4},{4,0},{8,12},{12,8},{16,20},{20,16},{24,28},{28,24},{1,5},{5... | collective-permute-start | bytes 9732104 | tf_op jit(solution)/shard_map/ppermute | solution.py:57
  222.8 10.3 %collective-permute-start.24 = (bf16[4,144,2560]{2,1,0:T(8,128)(2,1)}, bf16[4,144,2560]{2,1,0:T(8,128)(2,1)}, u32[]{:S(2)}, u32[]{:S(2)}) collective-permute-start(bf16[4,144,2560]{2,1,0:T(8,128)(2,1)} %get-tuple-element.340), channel_id=1, source_target_pairs={{0,4},{4,0},{8,12},{12,8},{16,20},{20,16},{24,28},{28,24},{1,5},{5... | collective-permute-start | bytes 8847368 | tf_op jit(solution)/shard_map/ppermute | solution.py:57
  241.4 37.8 %collective-permute-start.25 = (bf16[2,144,2816]{2,1,0:T(8,128)(2,1)}, bf16[2,144,2816]{2,1,0:T(8,128)(2,1)}, u32[]{:S(2)}, u32[]{:S(2)}) collective-permute-start(bf16[2,144,2816]{2,1,0:T(8,128)(2,1)} %get-tuple-element.384), channel_id=1, source_target_pairs={{0,8},{4,12},{8,0},{12,4},{16,24},{20,28},{24,16},{28,20},{1,9},{5... | collective-permute-start | bytes 4866056 | tf_op jit(solution)/shard_map/ppermute | solution.py:57
  241.9 34.4 %collective-permute-start.26 = (bf16[2,144,2560]{2,1,0:T(8,128)(2,1)}, bf16[2,144,2560]{2,1,0:T(8,128)(2,1)}, u32[]{:S(2)}, u32[]{:S(2)}) collective-permute-start(bf16[2,144,2560]{2,1,0:T(8,128)(2,1)} %get-tuple-element.385), channel_id=1, source_target_pairs={{0,16},{4,20},{8,24},{12,28},{16,0},{20,4},{24,8},{28,12},{1,17},{... | collective-permute-start | bytes 4423688 | tf_op jit(solution)/shard_map/ppermute | solution.py:57
  245.2 58.3 %all-to-all-start.2 = ((bf16[4,256,1152]{2,1,0:T(8,128)(2,1)}), bf16[4,256,1152]{2,1,0:T(8,128)(2,1)S(1)}, u32[]{:S(2)}, u32[]{:S(2)}) async-start(bf16[4,256,1152]{2,1,0:T(8,128)(2,1)} %pad_maximum_fusion.1), calls=%async_computation.2 | async-start | bytes 4718592 | tf_op jit(solution)/shard_map/all_to_all | solution.py:831
  261.0 18.7 %copy-start.16 = (bf16[2,144,2560]{2,1,0:T(8,128)(2,1)S(1)}, bf16[2,144,2560]{2,1,0:T(8,128)(2,1)}, u32[]{:S(2)}) copy-start(bf16[2,144,2560]{2,1,0:T(8,128)(2,1)} %get-tuple-element.390) | copy-start | bytes 4423684
  279.2 7.3 %collective-permute-start.27 = (bf16[4,144,1408]{2,1,0:T(8,128)(2,1)}, bf16[4,144,1408]{2,1,0:T(8,128)(2,1)S(1)}, u32[]{:S(2)}, u32[]{:S(2)}) collective-permute-start(bf16[4,144,1408]{2,1,0:T(8,128)(2,1)} %get-tuple-element.386), channel_id=1, source_target_pairs={{0,4},{4,0},{8,12},{12,8},{16,20},{20,16},{24,28},{28,24},{1,5},{5... | collective-permute-start | bytes 4866056 | tf_op jit(solution)/shard_map/ppermute | solution.py:57
  279.2 7.3 %collective-permute-start.28 = (bf16[4,144,1280]{2,1,0:T(8,128)(2,1)}, bf16[4,144,1280]{2,1,0:T(8,128)(2,1)S(1)}, u32[]{:S(2)}, u32[]{:S(2)}) collective-permute-start(bf16[4,144,1280]{2,1,0:T(8,128)(2,1)} %get-tuple-element.387), channel_id=1, source_target_pairs={{0,4},{4,0},{8,12},{12,8},{16,20},{20,16},{24,28},{28,24},{1,5},{5... | collective-permute-start | bytes 4423688 | tf_op jit(solution)/shard_map/ppermute | solution.py:57
  285.8 41.1 %collective-permute-start.31 = (bf16[144,2816]{1,0:T(8,128)(2,1)}, bf16[144,2816]{1,0:T(8,128)(2,1)}, u32[]{:S(2)}, u32[]{:S(2)}) collective-permute-start(bf16[144,2816]{1,0:T(8,128)(2,1)} %get-tuple-element.401), channel_id=1, source_target_pairs={{0,16},{4,20},{8,24},{12,28},{16,0},{20,4},{24,8},{28,12},{1,17},{... | collective-permute-start | bytes 2433032 | tf_op jit(solution)/shard_map/ppermute | solution.py:57
  290.8 36.1 %collective-permute-start.29 = (bf16[2,144,1408]{2,1,0:T(8,128)(2,1)}, bf16[2,144,1408]{2,1,0:T(8,128)(2,1)}, u32[]{:S(2)}, u32[]{:S(2)}) collective-permute-start(bf16[2,144,1408]{2,1,0:T(8,128)(2,1)} %get-tuple-element.397), channel_id=1, source_target_pairs={{0,8},{4,12},{8,0},{12,4},{16,24},{20,28},{24,16},{28,20},{1,9},{5... | collective-permute-start | bytes 2433032 | tf_op jit(solution)/shard_map/ppermute | solution.py:57
  291.5 35.3 %collective-permute-start.32 = (bf16[144,2560]{1,0:T(8,128)(2,1)}, bf16[144,2560]{1,0:T(8,128)(2,1)}, u32[]{:S(2)}, u32[]{:S(2)}) collective-permute-start(bf16[144,2560]{1,0:T(8,128)(2,1)} %get-tuple-element.402), channel_id=1, source_target_pairs={{0,8},{4,12},{8,0},{12,4},{16,24},{20,28},{24,16},{28,20},{1,9},{5... | collective-permute-start | bytes 2211848 | tf_op jit(solution)/shard_map/ppermute | solution.py:57
  292.8 34.0 %collective-permute-start.30 = (bf16[2,144,1280]{2,1,0:T(8,128)(2,1)}, bf16[2,144,1280]{2,1,0:T(8,128)(2,1)}, u32[]{:S(2)}, u32[]{:S(2)}) collective-permute-start(bf16[2,144,1280]{2,1,0:T(8,128)(2,1)} %get-tuple-element.398), channel_id=1, source_target_pairs={{0,16},{4,20},{8,24},{12,28},{16,0},{20,4},{24,8},{28,12},{1,17},{... | collective-permute-start | bytes 2211848 | tf_op jit(solution)/shard_map/ppermute | solution.py:57
  303.6 32.1 %all-to-all-start.3 = ((bf16[4,256,512]{2,1,0:T(8,128)(2,1)}), bf16[4,256,512]{2,1,0:T(8,128)(2,1)S(1)}, u32[]{:S(2)}, u32[]{:S(2)}) async-start(bf16[4,256,512]{2,1,0:T(8,128)(2,1)} %bitcast.60), calls=%async_computation.3 | async-start | bytes 2097152 | tf_op jit(solution)/shard_map/all_to_all | solution.py:868
  307.1 22.2 %copy-start.31 = (bf16[2,144,1408]{2,1,0:T(8,128)(2,1)S(1)}, bf16[2,144,1408]{2,1,0:T(8,128)(2,1)}, u32[]{:S(2)}) copy-start(bf16[2,144,1408]{2,1,0:T(8,128)(2,1)} %get-tuple-element.403) | copy-start | bytes 2433028
  331.6 11.3 %collective-permute-start.33 = (bf16[144,1408]{1,0:T(8,128)(2,1)}, bf16[144,1408]{1,0:T(8,128)(2,1)}, u32[]{:S(2)}, u32[]{:S(2)}) collective-permute-start(bf16[144,1408]{1,0:T(8,128)(2,1)} %get-tuple-element.410), channel_id=1, source_target_pairs={{0,16},{4,20},{8,24},{12,28},{16,0},{20,4},{24,8},{28,12},{1,17},{... | collective-permute-start | bytes 1216520 | tf_op jit(solution)/shard_map/ppermute | solution.py:57
  333.3 9.6 %collective-permute-start.34 = (bf16[144,1280]{1,0:T(8,128)(2,1)}, bf16[144,1280]{1,0:T(8,128)(2,1)}, u32[]{:S(2)}, u32[]{:S(2)}) collective-permute-start(bf16[144,1280]{1,0:T(8,128)(2,1)} %get-tuple-element.411), channel_id=1, source_target_pairs={{0,8},{4,12},{8,0},{12,4},{16,24},{20,28},{24,16},{28,20},{1,9},{5... | collective-permute-start | bytes 1105928 | tf_op jit(solution)/shard_map/ppermute | solution.py:57
  351.1 15.3 %collective-permute-start.38 = (bf16[36,640]{1,0:T(8,128)(2,1)S(1)}, bf16[36,640]{1,0:T(8,128)(2,1)S(1)}, u32[]{:S(2)}, u32[]{:S(2)}) collective-permute-start(bf16[36,640]{1,0:T(8,128)(2,1)S(1)} %get-tuple-element.522), channel_id=1, source_target_pairs={{0,1},{1,0},{2,3},{3,2},{4,5},{5,4},{6,7},{7,6},{8,9},{9,8},{10,11... | collective-permute-start | bytes 138248 | tf_op jit(solution)/shard_map/ppermute | solution.py:62
  351.6 15.5 %collective-permute-start.39 = (bf16[36,640]{1,0:T(8,128)(2,1)S(1)}, bf16[36,640]{1,0:T(8,128)(2,1)S(1)}, u32[]{:S(2)}, u32[]{:S(2)}) collective-permute-start(bf16[36,640]{1,0:T(8,128)(2,1)S(1)} %get-tuple-element.523), channel_id=1, source_target_pairs={{0,2},{1,3},{2,0},{3,1},{4,6},{5,7},{6,4},{7,5},{8,10},{9,11},{10,... | collective-permute-start | bytes 138248 | tf_op jit(solution)/shard_map/ppermute | solution.py:62
  354.9 12.2 %collective-permute-start.40 = (bf16[36,640]{1,0:T(8,128)(2,1)S(1)}, bf16[36,640]{1,0:T(8,128)(2,1)S(1)}, u32[]{:S(2)}, u32[]{:S(2)}) collective-permute-start(bf16[36,640]{1,0:T(8,128)(2,1)S(1)} %get-tuple-element.524), channel_id=1, source_target_pairs={{0,3},{1,2},{2,1},{3,0},{4,7},{5,6},{6,5},{7,4},{8,11},{9,10},{10,... | collective-permute-start | bytes 138248 | tf_op jit(solution)/shard_map/ppermute | solution.py:62
  355.6 16.4 %collective-permute-start.36 = (bf16[144,512]{1,0:T(8,128)(2,1)S(1)}, bf16[144,512]{1,0:T(8,128)(2,1)S(1)}, u32[]{:S(2)}, u32[]{:S(2)}) collective-permute-start(bf16[144,512]{1,0:T(8,128)(2,1)S(1)} %get-tuple-element.525), channel_id=1, source_target_pairs={{0,2},{1,3},{2,0},{3,1},{4,6},{5,7},{6,4},{7,5},{8,10},{9,11},{10,... | collective-permute-start | bytes 442376 | tf_op jit(solution)/shard_map/ppermute | solution.py:62
  356.5 15.5 %collective-permute-start.37 = (bf16[144,512]{1,0:T(8,128)(2,1)S(1)}, bf16[144,512]{1,0:T(8,128)(2,1)S(1)}, u32[]{:S(2)}, u32[]{:S(2)}) collective-permute-start(bf16[144,512]{1,0:T(8,128)(2,1)S(1)} %get-tuple-element.526), channel_id=1, source_target_pairs={{0,3},{1,2},{2,1},{3,0},{4,7},{5,6},{6,5},{7,4},{8,11},{9,10},{10,... | collective-permute-start | bytes 442376 | tf_op jit(solution)/shard_map/ppermute | solution.py:62
  366.5 5.5 %collective-permute-start.35 = (bf16[144,512]{1,0:T(8,128)(2,1)S(1)}, bf16[144,512]{1,0:T(8,128)(2,1)S(1)}, u32[]{:S(2)}, u32[]{:S(2)}) collective-permute-start(bf16[144,512]{1,0:T(8,128)(2,1)S(1)} %slice.350), channel_id=1, source_target_pairs={{0,1},{1,0},{2,3},{3,2},{4,5},{5,4},{6,7},{7,6},{8,9},{9,8},{10,11... | collective-permute-start | bytes 442376 | tf_op jit(solution)/shard_map/ppermute | solution.py:62
  (67 other events, 296.5 us)
